TPU v7x, 32 devices: a whole 2x2x4 slice. The times are simulated.
32 devices in a mesh: dp: 16 (over z, y, x), segment: 2 (over core).
Axes of the slice: x: 2, y: 2, z: 4, core: 2. Of those that a mesh axis runs over, the one named last changes fastest.
Arguments:
- latents: bfloat16 [16384, 640], P('dp'), may hold values from -6 to 6
- noise: bfloat16 [16384, 640], P('dp'), may hold values from -6 to 6
- timesteps: int32 [128], P('dp'), may hold values from 100 to 799
- reward_dir: float32 [640], replicated, may hold values from -6 to 6
- gain: float32 [2, 640], P('segment'), may hold values from 0.5 to 1.5
- time_scale: float32 [2, 640], P('segment'), may hold values from -6 to 6
- w_in: bfloat16 [2, 640, 640], P('segment', 'dp'), may hold values from -0.25 to 0.25
- w_out: bfloat16 [2, 640, 640], P('segment', 'dp'), may hold values from -0.25 to 0.25
Outputs:
- weight_grads: float32 [2, 640, 1280], P('segment', 'dp')
All inputs are finite; a program needn't handle non-finite values.
Results may differ from a plain program's by a relative error of at most 0.0004.
Values may be sent and summed in bfloat16 or wider, within the bound.
A program may use at most 64 MiB of HBM per device.

v0:
```python
import math

import jax
import jax.numpy as jnp
from jax import lax
from jax.sharding import PartitionSpec as P

GROUPS = 32
NSTEPS = 1000
STRIDE = 20


EPS = 1e-05


def passed_along(shard, axis, by):
    length = lax.axis_size(axis)
    pairs = [(i, i + by) for i in range(length) if 0 <= i + by < length]
    return lax.ppermute(shard, axis, pairs)


def group_norm(state_f32, group_count):
    channels = state_f32.shape[1]
    per_group = channels // group_count
    col_mean = jnp.mean(state_f32, axis=0)
    group_mean = jnp.repeat(jnp.mean(col_mean.reshape(group_count, per_group), axis=1), per_group)
    centered = state_f32 - group_mean
    sq_mean = jnp.mean(centered * centered, axis=0)
    variance = jnp.repeat(jnp.mean(sq_mean.reshape(group_count, per_group), axis=1), per_group)
    return centered * lax.rsqrt(variance + EPS)


def time_embed(timestep, channels):
    half_width = channels // 2
    frequencies = jnp.exp(
        -math.log(10000.0) * jnp.arange(half_width).astype(jnp.float32) / half_width
    )
    phases = timestep.astype(jnp.float32) * frequencies
    return jnp.concatenate([jnp.sin(phases), jnp.cos(phases)])


def alpha_bar(timestep):
    value = ((timestep.astype(jnp.float32) + 1.0) / NSTEPS + 0.008) / 1.008 * (math.pi / 2.0)
    return jnp.cos(value) ** 2


def contract_rows(left, right):
    return lax.dot_general(
        left, right, (((0,), (0,)), ((), ())), preferred_element_type=jnp.float32
    )


def contract_cols(left, right):
    return lax.dot_general(
        left, right, (((1,), (1,)), ((), ())), preferred_element_type=jnp.float32
    )


def block_forward(hidden, gain_row, temb, first, second):
    state_f32 = hidden.astype(jnp.float32)
    normed = (group_norm(state_f32, GROUPS) * gain_row).astype(jnp.bfloat16)
    preact = jnp.dot(normed, first, preferred_element_type=jnp.float32) + temb
    activation = jax.nn.silu(preact).astype(jnp.bfloat16)
    result = (state_f32 + jnp.dot(activation, second, preferred_element_type=jnp.float32)).astype(
        jnp.bfloat16
    )
    return (result, normed, preact, activation)


def block_backward(hidden, gain_row, preact, cotangent, first, second):
    grad_act = contract_cols(cotangent, second)
    gate_value = jax.nn.sigmoid(preact)
    grad_pre = (grad_act * gate_value * (1.0 + preact * (1.0 - gate_value))).astype(jnp.bfloat16)
    grad_norm = contract_cols(grad_pre, first)
    _, pullback = jax.vjp(lambda values: group_norm(values, GROUPS), hidden.astype(jnp.float32))
    new_cot = (cotangent.astype(jnp.float32) + pullback(grad_norm * gain_row)[0]).astype(
        jnp.bfloat16
    )
    return (new_cot, grad_pre)


def weight_term(normed, grad_pre, activation, cotangent):
    return jnp.concatenate(
        [contract_rows(normed, grad_pre), contract_rows(activation, cotangent)], axis=1
    )


def sample_head(hidden, latent, noise_block, timestep, reward_dir, loss_scale):
    ab_now = alpha_bar(timestep)
    ab_prev = alpha_bar(timestep - STRIDE)
    coef_a = jnp.sqrt(ab_now)
    coef_b = jnp.sqrt(1.0 - ab_now)
    coef_p = jnp.sqrt(ab_prev)
    coef_q = jnp.sqrt(0.75 * (1.0 - ab_prev))
    coef_r = 0.5 * jnp.sqrt(1.0 - ab_prev)
    noise_pred, pullback = jax.vjp(
        lambda values: group_norm(values, GROUPS), hidden.astype(jnp.float32)
    )
    current = latent.astype(jnp.float32)
    previous = (
        coef_p * (current - coef_b * noise_pred) / coef_a
        + coef_q * noise_pred
        + coef_r * noise_block.astype(jnp.float32)
    )
    squashed = jnp.tanh(previous)
    grad_pred = (
        (coef_q - coef_p * coef_b / coef_a) * reward_dir * (1.0 - squashed * squashed) * loss_scale
    )
    return pullback(grad_pred)[0].astype(jnp.bfloat16)


def put_slot(buffer, value, slot_index):
    return lax.dynamic_update_index_in_dim(buffer, value, slot_index, 0)


def body(latents, noise, timesteps, reward_dir, gain, time_scale, w_in, w_out):
    segments = lax.axis_size("segment")
    segment_index = lax.axis_index("segment")
    last_segment = segments - 1
    micro_count = timesteps.shape[0]
    crop_rows = latents.shape[0] // micro_count
    channels = latents.shape[1]
    loss_scale = 1.0 / math.sqrt(lax.axis_size("dp") * latents.shape[0])
    tick_count = micro_count + segments - 1
    whole_in, whole_out = (
        lax.all_gather(w_in, "dp", axis=1, tiled=True),
        lax.all_gather(w_out, "dp", axis=1, tiled=True),
    )
    first = whole_in[0]
    second = whole_out[0]
    gain_row = gain[0]
    latent_blocks = latents.reshape(micro_count, crop_rows, channels)
    noise_blocks = noise.reshape(micro_count, crop_rows, channels)
    embeds = jax.vmap(lambda values: time_embed(values, channels))(timesteps) * time_scale[0]
    blank = jnp.zeros((crop_rows, channels), jnp.bfloat16)
    blank_stack = jnp.zeros((micro_count, crop_rows, channels), jnp.bfloat16)
    stored = ()

    def forward_tick(tick_index, state_carry):
        incoming, inputs, head_cots, kept = state_carry
        micro_index = tick_index - segment_index
        active = (micro_index >= 0) & (micro_index < micro_count)
        slot_index = jnp.clip(micro_index, 0, micro_count - 1)
        fresh_input = latent_blocks[slot_index]
        hidden = jnp.where(segment_index == 0, fresh_input, incoming)

        def forward_compute(buffers):
            inputs, head_cots, kept = buffers
            result, normed, preact, activation = block_forward(
                hidden, gain_row, embeds[slot_index], first, second
            )
            inputs = put_slot(inputs, hidden, slot_index)
            head_cot = lax.cond(
                segment_index == last_segment,
                lambda: sample_head(
                    result,
                    fresh_input,
                    noise_blocks[slot_index],
                    timesteps[slot_index],
                    reward_dir,
                    loss_scale,
                ),
                lambda: blank,
            )
            head_cots = put_slot(head_cots, head_cot, slot_index)
            return (result, inputs, head_cots, kept)

        def forward_skipped(buffers):
            return (blank, buffers[0], buffers[1], buffers[2])

        result, inputs, head_cots, kept = lax.cond(
            active, forward_compute, forward_skipped, (inputs, head_cots, kept)
        )
        incoming = passed_along(result, "segment", 1)
        return (incoming, inputs, head_cots, kept)

    _, inputs, head_cots, kept = lax.fori_loop(
        0, tick_count, forward_tick, (blank, blank_stack, blank_stack, stored)
    )
    grad_start = ()
    records = (blank_stack, blank_stack, blank_stack, blank_stack)

    def backward_tick(tick_index, state_carry):
        incoming, grad_sum, records = state_carry
        micro_index = tick_index - (last_segment - segment_index)
        active = (micro_index >= 0) & (micro_index < micro_count)
        slot_index = jnp.clip(micro_index, 0, micro_count - 1)
        cotangent = jnp.where(segment_index == last_segment, head_cots[slot_index], incoming)

        def backward_compute(buffers):
            grad_sum, records = buffers
            hidden = inputs[slot_index]
            _, normed, preact, activation = block_forward(
                hidden, gain_row, embeds[slot_index], first, second
            )
            new_cot, grad_pre = block_backward(hidden, gain_row, preact, cotangent, first, second)
            records = (
                put_slot(records[0], normed, slot_index),
                put_slot(records[1], grad_pre, slot_index),
                put_slot(records[2], activation, slot_index),
                put_slot(records[3], cotangent, slot_index),
            )
            return (new_cot, grad_sum, records)

        def backward_skipped(buffers):
            return (blank, buffers[0], buffers[1])

        result, grad_sum, records = lax.cond(
            active, backward_compute, backward_skipped, (grad_sum, records)
        )
        incoming = passed_along(result, "segment", -1)
        return (incoming, grad_sum, records)

    _, grad_sum, records = lax.fori_loop(0, tick_count, backward_tick, (blank, grad_start, records))
    flat = [buffer.reshape(micro_count * crop_rows, channels) for buffer in records]
    full_terms = weight_term(flat[0], flat[1], flat[2], flat[3])
    grad_rows = lax.psum_scatter(full_terms, "dp", scatter_dimension=0, tiled=True)
    return grad_rows[None]


def solution(mesh):
    placed = (
        P("dp", None),
        P("dp", None),
        P("dp"),
        P(),
        P("segment", None),
        P("segment", None),
        P("segment", "dp", None),
        P("segment", "dp", None),
    )
    return jax.shard_map(
        body, mesh=mesh, in_specs=placed, out_specs=P("segment", "dp", None), check_vma=False
    )
```

profile of v0, /device:TPU:0, one launch (start us, length us, event | category | flops | bytes accessed | tf_op | source)
XLA Modules:
  0.0 441.2 jit_solution(14124167326209491752)
XLA Ops:
  7.2 47.4 %all_gather.6 = bf16[1,640,640]{2,1,0:T(8,128)(2,1)S(1)} all-gather(bf16[1,40,640]{2,1,0:T(8,128)(2,1)} %param.24), channel_id=1, replica_groups=mesh['dp'=16,'segment'=2] {'dp'}, dimensions={1}, use_global_device_ids=true | all-gather | bytes 870400 | tf_op jit(solution)/shard_map/all_gather | solution.py:126
  54.6 42.8 %all_gather.7 = bf16[1,640,640]{2,1,0:T(8,128)(2,1)} all-gather(bf16[1,40,640]{2,1,0:T(8,128)(2,1)} %param.25), channel_id=1, replica_groups=mesh['dp'=16,'segment'=2] {'dp'}, dimensions={1}, use_global_device_ids=true | all-gather | bytes 870400 | tf_op jit(solution)/shard_map/all_gather | solution.py:127
  99.0 151.2 %while.41 = (s32[]{:T(128)}, bf16[128,640]{1,0:T(8,128)(2,1)S(1)}, bf16[8,128,640]{2,1,0:T(8,128)(2,1)S(1)}, bf16[8,128,640]{2,1,0:T(8,128)(2,1)}, s32[]{:T(128)...) while((s32[]{:T(128)}, bf16[128,640]{1,0:T(8,128)(2,1)S(1)}, ...), condition=%wide.region_17.18_spmd, body=%wide.region_0.17_spmd.sunk | while | flops 214716976 | bytes 6583916 | solution.py:177
  99.1 5.1 %conditional.5 = (bf16[128,640]{1,0:T(8,128)(2,1)}, bf16[8,128,640]{2,1,0:T(8,128)(2,1)S(1)}, bf16[8,128,640]{2,1,0:T(8,128)(2,1)}) conditional(s32[]{:T(128)} %convert_element_type.261, (bf16[8,128,640]{2,1,0:T(8,128)(2,1)S(1)}, bf16[8,128,640]{2,1,0:T(8,128)(2,1)}) %tuple.119, (pred[]{:T(512)}, s32[]{:T(128)}, bf16[8,128,640]{2,1,0:T(8,128)(2,1)}, ...), branch_computations={%region_1.1_spmd, %region_2.16_spmd} | conditional | flops 214716976 | bytes 5928193 | solution.py:171
  111.8 11.6 %collective-permute-start = (bf16[128,640]{1,0:T(8,128)(2,1)}, bf16[128,640]{1,0:T(8,128)(2,1)S(1)}, u32[]{:S(2)}, u32[]{:S(2)}) collective-permute-start(bf16[128,640]{1,0:T(8,128)(2,1)} %get-tuple-element.1204), channel_id=1, source_target_pairs={{0,1},{2,3},{4,5},{6,7},{8,9},{10,11},{12,13},{14,15},{16,17},{18,... | collective-permute-start | bytes 491528 | tf_op jit(solution)/shard_map/while/body/eval_jaxpr/ppermute | solution.py:19
  129.7 11.6 %collective-permute-start = (bf16[128,640]{1,0:T(8,128)(2,1)}, bf16[128,640]{1,0:T(8,128)(2,1)S(1)}, u32[]{:S(2)}, u32[]{:S(2)}) collective-permute-start(bf16[128,640]{1,0:T(8,128)(2,1)} %get-tuple-element.1204), channel_id=1, source_target_pairs={{0,1},{2,3},{4,5},{6,7},{8,9},{10,11},{12,13},{14,15},{16,17},{18,... | collective-permute-start | bytes 491528 | tf_op jit(solution)/shard_map/while/body/eval_jaxpr/ppermute | solution.py:19
  147.7 11.6 %collective-permute-start = (bf16[128,640]{1,0:T(8,128)(2,1)}, bf16[128,640]{1,0:T(8,128)(2,1)S(1)}, u32[]{:S(2)}, u32[]{:S(2)}) collective-permute-start(bf16[128,640]{1,0:T(8,128)(2,1)} %get-tuple-element.1204), channel_id=1, source_target_pairs={{0,1},{2,3},{4,5},{6,7},{8,9},{10,11},{12,13},{14,15},{16,17},{18,... | collective-permute-start | bytes 491528 | tf_op jit(solution)/shard_map/while/body/eval_jaxpr/ppermute | solution.py:19
  165.6 11.6 %collective-permute-start = (bf16[128,640]{1,0:T(8,128)(2,1)}, bf16[128,640]{1,0:T(8,128)(2,1)S(1)}, u32[]{:S(2)}, u32[]{:S(2)}) collective-permute-start(bf16[128,640]{1,0:T(8,128)(2,1)} %get-tuple-element.1204), channel_id=1, source_target_pairs={{0,1},{2,3},{4,5},{6,7},{8,9},{10,11},{12,13},{14,15},{16,17},{18,... | collective-permute-start | bytes 491528 | tf_op jit(solution)/shard_map/while/body/eval_jaxpr/ppermute | solution.py:19
  178.5 5.1 %conditional.5 = (bf16[128,640]{1,0:T(8,128)(2,1)}, bf16[8,128,640]{2,1,0:T(8,128)(2,1)S(1)}, bf16[8,128,640]{2,1,0:T(8,128)(2,1)}) conditional(s32[]{:T(128)} %convert_element_type.261, (bf16[8,128,640]{2,1,0:T(8,128)(2,1)S(1)}, bf16[8,128,640]{2,1,0:T(8,128)(2,1)}) %tuple.119, (pred[]{:T(512)}, s32[]{:T(128)}, bf16[8,128,640]{2,1,0:T(8,128)(2,1)}, ...), branch_computations={%region_1.1_spmd, %region_2.16_spmd} | conditional | flops 214716976 | bytes 5928193 | solution.py:171
  183.6 11.6 %collective-permute-start = (bf16[128,640]{1,0:T(8,128)(2,1)}, bf16[128,640]{1,0:T(8,128)(2,1)S(1)}, u32[]{:S(2)}, u32[]{:S(2)}) collective-permute-start(bf16[128,640]{1,0:T(8,128)(2,1)} %get-tuple-element.1204), channel_id=1, source_target_pairs={{0,1},{2,3},{4,5},{6,7},{8,9},{10,11},{12,13},{14,15},{16,17},{18,... | collective-permute-start | bytes 491528 | tf_op jit(solution)/shard_map/while/body/eval_jaxpr/ppermute | solution.py:19
  201.5 11.7 %collective-permute-start = (bf16[128,640]{1,0:T(8,128)(2,1)}, bf16[128,640]{1,0:T(8,128)(2,1)S(1)}, u32[]{:S(2)}, u32[]{:S(2)}) collective-permute-start(bf16[128,640]{1,0:T(8,128)(2,1)} %get-tuple-element.1204), channel_id=1, source_target_pairs={{0,1},{2,3},{4,5},{6,7},{8,9},{10,11},{12,13},{14,15},{16,17},{18,... | collective-permute-start | bytes 491528 | tf_op jit(solution)/shard_map/while/body/eval_jaxpr/ppermute | solution.py:19
  219.5 11.6 %collective-permute-start = (bf16[128,640]{1,0:T(8,128)(2,1)}, bf16[128,640]{1,0:T(8,128)(2,1)S(1)}, u32[]{:S(2)}, u32[]{:S(2)}) collective-permute-start(bf16[128,640]{1,0:T(8,128)(2,1)} %get-tuple-element.1204), channel_id=1, source_target_pairs={{0,1},{2,3},{4,5},{6,7},{8,9},{10,11},{12,13},{14,15},{16,17},{18,... | collective-permute-start | bytes 491528 | tf_op jit(solution)/shard_map/while/body/eval_jaxpr/ppermute | solution.py:19
  233.0 16.0 %collective-permute-start = (bf16[128,640]{1,0:T(8,128)(2,1)}, bf16[128,640]{1,0:T(8,128)(2,1)S(1)}, u32[]{:S(2)}, u32[]{:S(2)}) collective-permute-start(bf16[128,640]{1,0:T(8,128)(2,1)} %get-tuple-element.1204), channel_id=1, source_target_pairs={{0,1},{2,3},{4,5},{6,7},{8,9},{10,11},{12,13},{14,15},{16,17},{18,... | collective-permute-start | bytes 491528 | tf_op jit(solution)/shard_map/while/body/eval_jaxpr/ppermute | solution.py:19
  255.0 86.7 %while.42 = (s32[]{:T(128)}, bf16[128,640]{1,0:T(8,128)(2,1)S(1)}, bf16[8,128,640]{2,1,0:T(8,128)(2,1)}, bf16[8,128,640]{2,1,0:T(8,128)(2,1)}, bf16[8,128,640]{2...) while((s32[]{:T(128)}, bf16[128,640]{1,0:T(8,128)(2,1)S(1)}, ...), condition=%wide.region_29.30_spmd, body=%wide.region_18.29_spmd.sunk | while | flops 318998528 | bytes 11287295 | solution.py:214
  256.3 7.6 %collective-permute-done.1 = bf16[128,640]{1,0:T(8,128)(2,1)S(1)} collective-permute-done((bf16[128,640]{1,0:T(8,128)(2,1)S(1)}, bf16[128,640]{1,0:T(8,128)(2,1)S(1)}, u32[]{:S(2)}, u32[]{:S(2)}) %collective-permute-start.1) | collective-permute-done | bytes 163872 | tf_op jit(solution)/shard_map/while/body/eval_jaxpr/ppermute | solution.py:19
  264.0 6.4 %conditional.6 = (bf16[128,640]{1,0:T(8,128)(2,1)S(1)}, bf16[8,128,640]{2,1,0:T(8,128)(2,1)}, bf16[8,128,640]{2,1,0:T(8,128)(2,1)}, bf16[8,128,640]{2,1,0:T(8,128)(2,1)}, bf16[8,128,640]{2,1,0:T(8,128)(2,1)}) conditional(s32[]{:T(128)} %convert_element_type.262, (bf16[8,128,640]{2,1,0:T(8,128)(2,1)}, bf16[8,128,640]{2,1,0:T(8,128)(2,1)}, ...), branch_computations={%region_19.19_spmd, %region_20.28_spmd} | conditional | flops 318998528 | bytes 10631564 | solution.py:208
  273.7 6.4 %conditional.6 = (bf16[128,640]{1,0:T(8,128)(2,1)S(1)}, bf16[8,128,640]{2,1,0:T(8,128)(2,1)}, bf16[8,128,640]{2,1,0:T(8,128)(2,1)}, bf16[8,128,640]{2,1,0:T(8,128)(2,1)}, bf16[8,128,640]{2,1,0:T(8,128)(2,1)}) conditional(s32[]{:T(128)} %convert_element_type.262, (bf16[8,128,640]{2,1,0:T(8,128)(2,1)}, bf16[8,128,640]{2,1,0:T(8,128)(2,1)}, ...), branch_computations={%region_19.19_spmd, %region_20.28_spmd} | conditional | flops 318998528 | bytes 10631564 | solution.py:208
  283.4 6.4 %conditional.6 = (bf16[128,640]{1,0:T(8,128)(2,1)S(1)}, bf16[8,128,640]{2,1,0:T(8,128)(2,1)}, bf16[8,128,640]{2,1,0:T(8,128)(2,1)}, bf16[8,128,640]{2,1,0:T(8,128)(2,1)}, bf16[8,128,640]{2,1,0:T(8,128)(2,1)}) conditional(s32[]{:T(128)} %convert_element_type.262, (bf16[8,128,640]{2,1,0:T(8,128)(2,1)}, bf16[8,128,640]{2,1,0:T(8,128)(2,1)}, ...), branch_computations={%region_19.19_spmd, %region_20.28_spmd} | conditional | flops 318998528 | bytes 10631564 | solution.py:208
  293.1 6.4 %conditional.6 = (bf16[128,640]{1,0:T(8,128)(2,1)S(1)}, bf16[8,128,640]{2,1,0:T(8,128)(2,1)}, bf16[8,128,640]{2,1,0:T(8,128)(2,1)}, bf16[8,128,640]{2,1,0:T(8,128)(2,1)}, bf16[8,128,640]{2,1,0:T(8,128)(2,1)}) conditional(s32[]{:T(128)} %convert_element_type.262, (bf16[8,128,640]{2,1,0:T(8,128)(2,1)}, bf16[8,128,640]{2,1,0:T(8,128)(2,1)}, ...), branch_computations={%region_19.19_spmd, %region_20.28_spmd} | conditional | flops 318998528 | bytes 10631564 | solution.py:208
  302.8 6.4 %conditional.6 = (bf16[128,640]{1,0:T(8,128)(2,1)S(1)}, bf16[8,128,640]{2,1,0:T(8,128)(2,1)}, bf16[8,128,640]{2,1,0:T(8,128)(2,1)}, bf16[8,128,640]{2,1,0:T(8,128)(2,1)}, bf16[8,128,640]{2,1,0:T(8,128)(2,1)}) conditional(s32[]{:T(128)} %convert_element_type.262, (bf16[8,128,640]{2,1,0:T(8,128)(2,1)}, bf16[8,128,640]{2,1,0:T(8,128)(2,1)}, ...), branch_computations={%region_19.19_spmd, %region_20.28_spmd} | conditional | flops 318998528 | bytes 10631564 | solution.py:208
  312.5 6.4 %conditional.6 = (bf16[128,640]{1,0:T(8,128)(2,1)S(1)}, bf16[8,128,640]{2,1,0:T(8,128)(2,1)}, bf16[8,128,640]{2,1,0:T(8,128)(2,1)}, bf16[8,128,640]{2,1,0:T(8,128)(2,1)}, bf16[8,128,640]{2,1,0:T(8,128)(2,1)}) conditional(s32[]{:T(128)} %convert_element_type.262, (bf16[8,128,640]{2,1,0:T(8,128)(2,1)}, bf16[8,128,640]{2,1,0:T(8,128)(2,1)}, ...), branch_computations={%region_19.19_spmd, %region_20.28_spmd} | conditional | flops 318998528 | bytes 10631564 | solution.py:208
  322.3 6.4 %conditional.6 = (bf16[128,640]{1,0:T(8,128)(2,1)S(1)}, bf16[8,128,640]{2,1,0:T(8,128)(2,1)}, bf16[8,128,640]{2,1,0:T(8,128)(2,1)}, bf16[8,128,640]{2,1,0:T(8,128)(2,1)}, bf16[8,128,640]{2,1,0:T(8,128)(2,1)}) conditional(s32[]{:T(128)} %convert_element_type.262, (bf16[8,128,640]{2,1,0:T(8,128)(2,1)}, bf16[8,128,640]{2,1,0:T(8,128)(2,1)}, ...), branch_computations={%region_19.19_spmd, %region_20.28_spmd} | conditional | flops 318998528 | bytes 10631564 | solution.py:208
  332.0 6.4 %conditional.6 = (bf16[128,640]{1,0:T(8,128)(2,1)S(1)}, bf16[8,128,640]{2,1,0:T(8,128)(2,1)}, bf16[8,128,640]{2,1,0:T(8,128)(2,1)}, bf16[8,128,640]{2,1,0:T(8,128)(2,1)}, bf16[8,128,640]{2,1,0:T(8,128)(2,1)}) conditional(s32[]{:T(128)} %convert_element_type.262, (bf16[8,128,640]{2,1,0:T(8,128)(2,1)}, bf16[8,128,640]{2,1,0:T(8,128)(2,1)}, ...), branch_computations={%region_19.19_spmd, %region_20.28_spmd} | conditional | flops 318998528 | bytes 10631564 | solution.py:208
  349.3 83.0 %reduce-scatter.4.cloned.1.call-done = f32[40,1280]{1,0:T(8,128)} async-done(((f32[640,1280]{1,0:T(8,128)}), f32[40,1280]{1,0:T(8,128)}) %reduce-scatter.4.cloned.1.call-update) | async-done | bytes 204816
  (510 shorter events, 178.8 us)
Async XLA Ops:
  6.5 90.9 %copy-start.5 = (f32[1,640]{1,0:T(1,128)S(1)}, f32[1,640]{1,0:T(1,128)}, u32[]{:S(2)}) copy-start(f32[1,640]{1,0:T(1,128)} %param.23) | copy-start | bytes 7684
  6.5 425.8 %reduce-scatter.4.cloned.1.call-start = ((), (), s32[]{:S(2)}) async-start(), calls=%async_computation.1 | async-start | bytes 3481600
  97.7 1.4 copy-start.3
  97.7 1.4 copy-start.4
  104.2 2.5 collective-permute-start
  111.8 12.8 %collective-permute-start = (bf16[128,640]{1,0:T(8,128)(2,1)}, bf16[128,640]{1,0:T(8,128)(2,1)S(1)}, u32[]{:S(2)}, u32[]{:S(2)}) collective-permute-start(bf16[128,640]{1,0:T(8,128)(2,1)} %get-tuple-element.1204), channel_id=1, source_target_pairs={{0,1},{2,3},{4,5},{6,7},{8,9},{10,11},{12,13},{14,15},{16,17},{18,... | collective-permute-start | bytes 491528 | tf_op jit(solution)/shard_map/while/body/eval_jaxpr/ppermute | solution.py:19
  129.7 12.8 %collective-permute-start = (bf16[128,640]{1,0:T(8,128)(2,1)}, bf16[128,640]{1,0:T(8,128)(2,1)S(1)}, u32[]{:S(2)}, u32[]{:S(2)}) collective-permute-start(bf16[128,640]{1,0:T(8,128)(2,1)} %get-tuple-element.1204), channel_id=1, source_target_pairs={{0,1},{2,3},{4,5},{6,7},{8,9},{10,11},{12,13},{14,15},{16,17},{18,... | collective-permute-start | bytes 491528 | tf_op jit(solution)/shard_map/while/body/eval_jaxpr/ppermute | solution.py:19
  147.7 12.8 %collective-permute-start = (bf16[128,640]{1,0:T(8,128)(2,1)}, bf16[128,640]{1,0:T(8,128)(2,1)S(1)}, u32[]{:S(2)}, u32[]{:S(2)}) collective-permute-start(bf16[128,640]{1,0:T(8,128)(2,1)} %get-tuple-element.1204), channel_id=1, source_target_pairs={{0,1},{2,3},{4,5},{6,7},{8,9},{10,11},{12,13},{14,15},{16,17},{18,... | collective-permute-start | bytes 491528 | tf_op jit(solution)/shard_map/while/body/eval_jaxpr/ppermute | solution.py:19
  165.6 12.8 %collective-permute-start = (bf16[128,640]{1,0:T(8,128)(2,1)}, bf16[128,640]{1,0:T(8,128)(2,1)S(1)}, u32[]{:S(2)}, u32[]{:S(2)}) collective-permute-start(bf16[128,640]{1,0:T(8,128)(2,1)} %get-tuple-element.1204), channel_id=1, source_target_pairs={{0,1},{2,3},{4,5},{6,7},{8,9},{10,11},{12,13},{14,15},{16,17},{18,... | collective-permute-start | bytes 491528 | tf_op jit(solution)/shard_map/while/body/eval_jaxpr/ppermute | solution.py:19
  183.6 12.8 %collective-permute-start = (bf16[128,640]{1,0:T(8,128)(2,1)}, bf16[128,640]{1,0:T(8,128)(2,1)S(1)}, u32[]{:S(2)}, u32[]{:S(2)}) collective-permute-start(bf16[128,640]{1,0:T(8,128)(2,1)} %get-tuple-element.1204), channel_id=1, source_target_pairs={{0,1},{2,3},{4,5},{6,7},{8,9},{10,11},{12,13},{14,15},{16,17},{18,... | collective-permute-start | bytes 491528 | tf_op jit(solution)/shard_map/while/body/eval_jaxpr/ppermute | solution.py:19
  201.5 12.9 %collective-permute-start = (bf16[128,640]{1,0:T(8,128)(2,1)}, bf16[128,640]{1,0:T(8,128)(2,1)S(1)}, u32[]{:S(2)}, u32[]{:S(2)}) collective-permute-start(bf16[128,640]{1,0:T(8,128)(2,1)} %get-tuple-element.1204), channel_id=1, source_target_pairs={{0,1},{2,3},{4,5},{6,7},{8,9},{10,11},{12,13},{14,15},{16,17},{18,... | collective-permute-start | bytes 491528 | tf_op jit(solution)/shard_map/while/body/eval_jaxpr/ppermute | solution.py:19
  219.5 12.8 %collective-permute-start = (bf16[128,640]{1,0:T(8,128)(2,1)}, bf16[128,640]{1,0:T(8,128)(2,1)S(1)}, u32[]{:S(2)}, u32[]{:S(2)}) collective-permute-start(bf16[128,640]{1,0:T(8,128)(2,1)} %get-tuple-element.1204), channel_id=1, source_target_pairs={{0,1},{2,3},{4,5},{6,7},{8,9},{10,11},{12,13},{14,15},{16,17},{18,... | collective-permute-start | bytes 491528 | tf_op jit(solution)/shard_map/while/body/eval_jaxpr/ppermute | solution.py:19
  233.0 17.3 %collective-permute-start = (bf16[128,640]{1,0:T(8,128)(2,1)}, bf16[128,640]{1,0:T(8,128)(2,1)S(1)}, u32[]{:S(2)}, u32[]{:S(2)}) collective-permute-start(bf16[128,640]{1,0:T(8,128)(2,1)} %get-tuple-element.1204), channel_id=1, source_target_pairs={{0,1},{2,3},{4,5},{6,7},{8,9},{10,11},{12,13},{14,15},{16,17},{18,... | collective-permute-start | bytes 491528 | tf_op jit(solution)/shard_map/while/body/eval_jaxpr/ppermute | solution.py:19
  255.0 8.9 %collective-permute-start.1 = (bf16[128,640]{1,0:T(8,128)(2,1)S(1)}, bf16[128,640]{1,0:T(8,128)(2,1)S(1)}, u32[]{:S(2)}, u32[]{:S(2)}) collective-permute-start(bf16[128,640]{1,0:T(8,128)(2,1)S(1)} %get-tuple-element.1221), channel_id=1, source_target_pairs={{1,0},{3,2},{5,4},{7,6},{9,8},{11,10},{13,12},{15,14},{17,16},{19,... | collective-permute-start | bytes 491528 | tf_op jit(solution)/shard_map/while/body/eval_jaxpr/ppermute | solution.py:19
  270.4 3.3 collective-permute-start.1
  280.1 3.3 collective-permute-start.1
  289.8 3.3 collective-permute-start.1
  299.5 3.3 collective-permute-start.1
  309.3 3.3 collective-permute-start.1
  319.0 3.3 collective-permute-start.1
  328.7 3.3 collective-permute-start.1
  338.4 3.3 collective-permute-start.1
  341.7 3.1 copy-start
  341.7 3.1 copy-start.1
  (9 other events, 10.5 us)
Sparse Core Ops, SparseCore 0:
  349.5 82.7 reduce-scatter.3
where the time goes:
time: 444 us; the launch traced here: 441 us
  waiting for transfers between devices  117 us (26%)
  starting transfers between devices  110 us (25%)
  blocking collectives  90.2 us (20%)
  matrix products  43.1 us (10%)
  other arithmetic  32.7 us (7%)
  local copies, waits for them, and re-layouts  31.9 us (7%)
  between operations  13.5 us (3%)
    ppermute x18, starting transfers between devices, passed_along(): return lax.ppermute(shard, axis, pairs)  110 us
    unnamed x2, waiting for transfers between devices  83 us
    all_gather x1, blocking collectives, body(): lax.all_gather(w_in, 'dp', axis=1, tiled=True)  47.4 us
    all_gather x1, blocking collectives, body(): lax.all_gather(w_out, 'dp', axis=1, tiled=True)  42.8 us
    ppermute x18, waiting for transfers between devices, passed_along(): return lax.ppermute(shard, axis, pairs)  34.4 us
    dynamic_update_slice x16, other arithmetic, put_slot(): return lax.dynamic_update_index_in_dim(buffer, value, slot_index, 0)  21.7 us
    dot_general x8, matrix products, block_forward(): jnp.dot(activation, second, preferred_element_type=jnp.float32)  19.2 us
    dot_general x16, matrix products, contract_cols(): lax.dot_general(left, right, (((1,), (1,)), ((), ())), preferred_element_...  11.3 us
  transfers between devices with their start and end apart: 19, of which 19 were waited for; matrix products, arithmetic and copies ran while one was open for 0% of the time, Pallas kernels for 0%

commit v1 on v0

--- a/solution.py
+++ b/solution.py
@@ -1,8 +1,11 @@
+import functools
 import math
 
 import jax
 import jax.numpy as jnp
 from jax import lax
+from jax.experimental import pallas as pl
+from jax.experimental.pallas import tpu as pltpu
 from jax.sharding import PartitionSpec as P
 
 GROUPS = 32
@@ -218,6 +221,431 @@
     return grad_rows[None]
 
 
+def split_rows(values):
+    high = values.astype(jnp.bfloat16).astype(jnp.float32)
+    rest = values - high
+    middle = rest.astype(jnp.bfloat16).astype(jnp.float32)
+    low = rest - middle
+    return jnp.concatenate([high, middle, low], axis=0).astype(jnp.bfloat16)
+
+
+def step_kernel(
+    shape,
+    shard_ref,
+    param_ref,
+    latent_ref,
+    noise_ref,
+    embed_ref,
+    reward_ref,
+    coef_ref,
+    out_ref,
+    wbuf,
+    pbuf,
+    weights,
+    states,
+    normed,
+    slopes,
+    acts,
+    cots,
+    gradpre,
+    means,
+    scales,
+    sums,
+    spread,
+    gather_mat,
+    scatter_mat,
+    grads,
+    inbox0,
+    inbox1,
+    inbox2,
+    inbox3,
+    send_sem,
+    recv_sem,
+    local_sem,
+):
+    dp, depth, shard, channels, images, rows, loss_scale = shape
+    me = lax.axis_index("dp")
+    core = lax.axis_index("segment")
+    other = 1 - core
+    col = lax.rem(me, 4)
+    z = me // 4
+    qx = col + 1 - 2 * lax.rem(col, 2)
+    qy = lax.rem(col + 2, 4)
+    qd = 3 - col
+    x_dev = (z * 4 + qx, core)
+    y_dev = (z * 4 + qy, core)
+    partner = (me, other)
+    z_at = [lax.rem(z + dz, depth) for dz in range(depth)]
+    z_from = [lax.rem(z + depth - dz, depth) for dz in range(depth)]
+    z_dev = [(z_at[dz] * 4 + col, core) for dz in range(depth)]
+    count = [0]
+    pending = []
+
+    def remote(src, dst, device):
+        k = count[0]
+        count[0] += 1
+        copy = pltpu.make_async_remote_copy(
+            src_ref=src,
+            dst_ref=dst,
+            send_sem=send_sem.at[k],
+            recv_sem=recv_sem.at[k],
+            device_id=device,
+            device_id_type=pl.DeviceIdType.MESH,
+        )
+        copy.start()
+        pending.append(copy)
+        return copy
+
+    barrier = pltpu.get_barrier_semaphore()
+    friends = [x_dev, y_dev, partner] + z_dev[1:]
+    for device in friends:
+        pl.semaphore_signal(
+            barrier, inc=1, device_id=device, device_id_type=pl.DeviceIdType.MESH
+        )
+    pl.semaphore_wait(barrier, len(friends))
+
+    own = pltpu.make_async_copy(shard_ref, wbuf.at[core, col, z], local_sem.at[0])
+    own.start()
+    own_param = pltpu.make_async_copy(param_ref, pbuf.at[core], local_sem.at[1])
+    own_param.start()
+
+    to_z = [None] + [
+        remote(shard_ref, wbuf.at[core, col, z], z_dev[dz]) for dz in range(1, depth)
+    ]
+    to_x = [remote(shard_ref, wbuf.at[core, col, z], x_dev)]
+    to_y = [remote(shard_ref, wbuf.at[core, col, z], y_dev)]
+    to_core = [
+        remote(shard_ref, wbuf.at[core, col, z], partner),
+        remote(param_ref, pbuf.at[core], partner),
+    ]
+    ch = lax.broadcasted_iota(jnp.int32, gather_mat.shape, 0)
+    gr = lax.broadcasted_iota(jnp.int32, gather_mat.shape, 1) * (channels // GROUPS)
+    inside = (ch >= gr) & (ch < gr + channels // GROUPS)
+    gather_mat[...] = jnp.where(inside, 1.0, 0.0).astype(jnp.bfloat16)
+    ch = lax.broadcasted_iota(jnp.int32, scatter_mat.shape, 1)
+    gr = lax.broadcasted_iota(jnp.int32, scatter_mat.shape, 0) * (channels // GROUPS)
+    inside = (ch >= gr) & (ch < gr + channels // GROUPS)
+    scatter_mat[...] = jnp.where(inside, 1.0, 0.0).astype(jnp.bfloat16)
+    sums[...] = jnp.zeros_like(sums)
+
+    for dz in range(1, depth):
+        to_z[dz].wait_recv()
+        piece = wbuf.at[core, col, z_from[dz]]
+        to_x.append(remote(piece, piece, x_dev))
+        to_y.append(remote(piece, piece, y_dev))
+        to_core.append(remote(piece, piece, partner))
+    second = []
+    for dz in range(depth):
+        to_x[dz].wait_recv()
+        to_y[dz].wait_recv()
+        from_x = wbuf.at[core, qx, z_from[dz]]
+        from_y = wbuf.at[core, qy, z_from[dz]]
+        half_in, half_out = from_x.at[0], from_y.at[1]
+        second.append(remote(half_in, half_in, y_dev))
+        second.append(remote(half_out, half_out, x_dev))
+        to_core.append(remote(from_x, from_x, partner))
+        to_core.append(remote(from_y, from_y, partner))
+    for dz in range(depth):
+        second[2 * dz].wait_recv()
+        second[2 * dz + 1].wait_recv()
+        piece = wbuf.at[core, qd, z_from[dz]]
+        to_core.append(remote(piece, piece, partner))
+    own.wait()
+    own_param.wait()
+    for copy in to_core:
+        copy.wait_recv()
+
+    for section in range(2):
+        for kind in range(2):
+            for pair in range(dp // 2):
+                q, zz = (2 * pair) % 4, pair // 2
+                both = jnp.concatenate(
+                    [
+                        wbuf[section, q, zz, kind].astype(jnp.float32),
+                        wbuf[section, q + 1, zz, kind].astype(jnp.float32),
+                    ],
+                    axis=0,
+                )
+                weights[section, kind, 2 * pair * shard : 2 * (pair + 1) * shard, :] = (
+                    both.astype(jnp.bfloat16)
+                )
+
+    def group_means(values):
+        parts = jnp.dot(
+            split_rows(values), gather_mat[...], preferred_element_type=jnp.float32
+        )
+        lines = values.shape[0]
+        total = parts[:lines] + parts[lines : 2 * lines] + parts[2 * lines :]
+        total = total * (1.0 / (rows * (channels // GROUPS)))
+        parts = jnp.dot(
+            split_rows(total), scatter_mat[...], preferred_element_type=jnp.float32
+        )
+        return parts[:lines] + parts[lines : 2 * lines] + parts[2 * lines :]
+
+    def statistics(stage):
+        def mean_body(i, carry):
+            block = states[stage, pl.ds(i * rows, rows), :].astype(jnp.float32)
+            sums[pl.ds(i, 1), :] = jnp.sum(block, axis=0, keepdims=True)
+            return carry
+
+        lax.fori_loop(0, images, mean_body, 0)
+        means[stage] = group_means(sums[...])
+
+        def square_body(i, carry):
+            block = states[stage, pl.ds(i * rows, rows), :].astype(jnp.float32)
+            centered = block - means[stage, pl.ds(i, 1), :]
+            sums[pl.ds(i, 1), :] = jnp.sum(centered * centered, axis=0, keepdims=True)
+            return carry
+
+        lax.fori_loop(0, images, square_body, 0)
+        scales[stage] = lax.rsqrt(group_means(sums[...]) + EPS)
+
+    def unit(stage, i):
+        block = states[stage, pl.ds(i * rows, rows), :].astype(jnp.float32)
+        return (block - means[stage, pl.ds(i, 1), :]) * scales[stage, pl.ds(i, 1), :]
+
+    joint = 2 if images % 2 == 0 else 1
+    base = core * (images * rows)
+
+    def load_body(i, carry):
+        where = pl.ds(pl.multiple_of(i * rows, rows), rows)
+        states[0, where, :] = latent_ref[
+            pl.ds(pl.multiple_of(base + i * rows, rows), rows), :
+        ]
+        return carry
+
+    lax.fori_loop(0, images, load_body, 0)
+
+    for section in range(2):
+        statistics(section)
+        gain_row = pbuf[section, 0:1, :]
+        time_row = pbuf[section, 1:2, :]
+
+        def forward_body(g, carry):
+            for j in range(joint):
+                i = g * joint + j
+                where = pl.ds(pl.multiple_of(i * rows, rows), rows)
+                normed[section, where, :] = (unit(section, i) * gain_row).astype(jnp.bfloat16)
+            span = pl.ds(pl.multiple_of(g * joint * rows, rows), joint * rows)
+            product = jnp.dot(
+                normed[section, span, :],
+                weights[section, 0],
+                preferred_element_type=jnp.float32,
+            )
+            for j in range(joint):
+                i = g * joint + j
+                where = pl.ds(pl.multiple_of(i * rows, rows), rows)
+                preact = product[j * rows : (j + 1) * rows] + time_row * embed_ref[pl.ds(i, 1), :]
+                gate = jax.nn.sigmoid(preact)
+                acts[section, where, :] = (preact * gate).astype(jnp.bfloat16)
+                slopes[section, where, :] = gate * (1.0 + preact * (1.0 - gate))
+            product = jnp.dot(
+                acts[section, span, :],
+                weights[section, 1],
+                preferred_element_type=jnp.float32,
+            )
+            states[section + 1, span, :] = (
+                states[section, span, :].astype(jnp.float32) + product
+            ).astype(jnp.bfloat16)
+            return carry
+
+        lax.fori_loop(0, images // joint, forward_body, 0)
+
+    statistics(2)
+
+    def head_body(i, carry):
+        where = pl.ds(pl.multiple_of(i * rows, rows), rows)
+        pred = unit(2, i)
+        current = states[0, where, :].astype(jnp.float32)
+        fresh = noise_ref[pl.ds(pl.multiple_of(base + i * rows, rows), rows), :].astype(
+            jnp.float32
+        )
+        keep, pull, stir = coef_ref[0, i], coef_ref[1, i], coef_ref[2, i]
+        squashed = jnp.tanh(keep * current + pull * pred + stir * fresh)
+        grad = (1.0 - squashed * squashed) * (reward_ref[...] * (pull * loss_scale))
+        spread[where, :] = grad
+        sums[pl.ds(i, 1), :] = jnp.sum(grad, axis=0, keepdims=True)
+        sums[pl.ds(images + i, 1), :] = jnp.sum(grad * pred, axis=0, keepdims=True)
+        return carry
+
+    lax.fori_loop(0, images, head_body, 0)
+
+    def pull_back(stage, incoming):
+        means_two = group_means(sums[...])
+        sums[...] = means_two
+
+        def body(i, carry):
+            where = pl.ds(pl.multiple_of(i * rows, rows), rows)
+            pulled = scales[stage, pl.ds(i, 1), :] * (
+                spread[where, :]
+                - sums[pl.ds(i, 1), :]
+                - unit(stage, i) * sums[pl.ds(images + i, 1), :]
+            )
+            if incoming is not None:
+                pulled = cots[incoming, where, :].astype(jnp.float32) + pulled
+            cots[stage - 1, where, :] = pulled.astype(jnp.bfloat16)
+            return carry
+
+        lax.fori_loop(0, images, body, 0)
+
+    pull_back(2, None)
+
+    for section in (1, 0):
+        gain_row = pbuf[section, 0:1, :]
+
+        def backward_body(g, carry):
+            span = pl.ds(pl.multiple_of(g * joint * rows, rows), joint * rows)
+            product = contract_cols(cots[section, span, :], weights[section, 1])
+            gradpre[section, span, :] = (product * slopes[section, span, :]).astype(jnp.bfloat16)
+            if section > 0:
+                product = contract_cols(gradpre[section, span, :], weights[section, 0])
+                for j in range(joint):
+                    i = g * joint + j
+                    where = pl.ds(pl.multiple_of(i * rows, rows), rows)
+                    grad = product[j * rows : (j + 1) * rows] * gain_row
+                    spread[where, :] = grad
+                    sums[pl.ds(i, 1), :] = jnp.sum(grad, axis=0, keepdims=True)
+                    sums[pl.ds(images + i, 1), :] = jnp.sum(
+                        grad * unit(section, i), axis=0, keepdims=True
+                    )
+            return carry
+
+        lax.fori_loop(0, images // joint, backward_body, 0)
+        if section > 0:
+            pull_back(section, section)
+        for kind in range(2):
+            if kind == 0:
+                term = contract_rows(normed[section], gradpre[section])
+            else:
+                term = contract_rows(acts[section], cots[section])
+            for owner in range(dp):
+                grads[section, kind, owner % 4, owner // 4] = term[
+                    owner * shard : (owner + 1) * shard
+                ]
+
+    def add(kind, q, values_ref):
+        def body(k, carry):
+            grads[core, kind, q, k] = grads[core, kind, q, k] + values_ref[k]
+            return carry
+
+        lax.fori_loop(0, depth, body, 0)
+
+    order = ((qd, qd), (qx, qy), (qy, qx), (col, col))
+    swaps = {}
+    for step in range(4):
+        for kind in range(2):
+            q = order[step][kind]
+            swaps[step, kind] = remote(
+                grads.at[other, kind, q], inbox0.at[kind, q], partner
+            )
+    first = {}
+    final = {}
+    cross = ((x_dev, qx, qy), (y_dev, qy, qx))
+    for step in range(2):
+        for kind in range(2):
+            q = order[step][kind]
+            swaps[step, kind].wait_recv()
+            add(kind, q, inbox0.at[kind, q])
+            first[step, kind] = remote(
+                grads.at[core, kind, q], inbox1.at[kind, step], cross[kind][0]
+            )
+    for kind in range(2):
+        q = order[2][kind]
+        swaps[2, kind].wait_recv()
+        add(kind, q, inbox0.at[kind, q])
+        first[0, kind].wait_recv()
+        add(kind, q, inbox1.at[kind, 0])
+        final[kind] = remote(grads.at[core, kind, q], inbox2.at[kind], cross[1 - kind][0])
+    last = {}
+    for kind in range(2):
+        swaps[3, kind].wait_recv()
+        add(kind, col, inbox0.at[kind, col])
+        first[1, kind].wait_recv()
+        add(kind, col, inbox1.at[kind, 1])
+        final[kind].wait_recv()
+        add(kind, col, inbox2.at[kind])
+        for dz in range(1, depth):
+            last[kind, dz] = remote(
+                grads.at[core, kind, col, z_at[dz]], inbox3.at[kind, dz], z_dev[dz]
+            )
+    for kind in range(2):
+        total = grads[core, kind, col, z]
+        for dz in range(1, depth):
+            last[kind, dz].wait_recv()
+            total = total + inbox3[kind, dz]
+        out_ref[:, kind * channels : (kind + 1) * channels] = total
+    for copy in pending:
+        copy.wait_send()
+
+
+def fused_body(latents, noise, timesteps, reward_dir, gain, time_scale, w_in, w_out):
+    dp = lax.axis_size("dp")
+    depth = dp // 4
+    core = lax.axis_index("segment")
+    micro_count = timesteps.shape[0]
+    images = micro_count // 2
+    rows = latents.shape[0] // micro_count
+    channels = latents.shape[1]
+    shard = w_in.shape[1]
+    loss_scale = 1.0 / math.sqrt(dp * latents.shape[0])
+    times = lax.dynamic_slice_in_dim(timesteps, core * images, images)
+    embeds = jax.vmap(lambda values: time_embed(values, channels))(times)
+    ab_now, ab_prev = alpha_bar(times), alpha_bar(times - STRIDE)
+    coef_a, coef_b = jnp.sqrt(ab_now), jnp.sqrt(1.0 - ab_now)
+    coef_p, coef_q = jnp.sqrt(ab_prev), jnp.sqrt(0.75 * (1.0 - ab_prev))
+    coefs = jnp.stack(
+        [coef_p / coef_a, coef_q - coef_p * coef_b / coef_a, 0.5 * jnp.sqrt(1.0 - ab_prev)]
+    )
+    shards = jnp.concatenate([w_in, w_out], axis=0)
+    params = jnp.concatenate([gain, time_scale, jnp.zeros((6, channels), jnp.float32)], axis=0)
+    shape = (dp, depth, shard, channels, images, rows, loss_scale)
+    total_rows = images * rows
+    bf16, f32 = jnp.bfloat16, jnp.float32
+    lines = -(-2 * images // 8) * 8
+    square = (shard, channels)
+    copies = 96 * depth
+    vmem = pl.BlockSpec(memory_space=pltpu.VMEM)
+    grad_rows = pl.pallas_call(
+        functools.partial(step_kernel, shape),
+        out_shape=jax.ShapeDtypeStruct((shard, 2 * channels), f32),
+        in_specs=[vmem] * 6 + [pl.BlockSpec(memory_space=pltpu.SMEM)],
+        out_specs=vmem,
+        scratch_shapes=[
+            pltpu.VMEM((2, 4, depth, 2) + square, bf16),
+            pltpu.VMEM((2, 8, channels), f32),
+            pltpu.VMEM((2, 2, channels, channels), bf16),
+            pltpu.VMEM((3, total_rows, channels), bf16),
+            pltpu.VMEM((2, total_rows, channels), bf16),
+            pltpu.VMEM((2, total_rows, channels), f32),
+            pltpu.VMEM((2, total_rows, channels), bf16),
+            pltpu.VMEM((2, total_rows, channels), bf16),
+            pltpu.VMEM((2, total_rows, channels), bf16),
+            pltpu.VMEM((3, lines, channels), f32),
+            pltpu.VMEM((3, lines, channels), f32),
+            pltpu.VMEM((lines, channels), f32),
+            pltpu.VMEM((total_rows, channels), f32),
+            pltpu.VMEM((channels, 128), bf16),
+            pltpu.VMEM((128, channels), bf16),
+            pltpu.VMEM((2, 2, 4, depth) + square, f32),
+            pltpu.VMEM((2, 4, depth) + square, f32),
+            pltpu.VMEM((2, 2, depth) + square, f32),
+            pltpu.VMEM((2, depth) + square, f32),
+            pltpu.VMEM((2, depth) + square, f32),
+            pltpu.SemaphoreType.DMA((copies,)),
+            pltpu.SemaphoreType.DMA((copies,)),
+            pltpu.SemaphoreType.DMA((2,)),
+        ],
+        compiler_params=pltpu.CompilerParams(
+            collective_id=0, has_side_effects=True, vmem_limit_bytes=60 * 1024 * 1024
+        ),
+    )(shards, params, latents, noise, embeds, reward_dir[None], coefs)
+    return grad_rows[None]
+
+
+def fits(mesh):
+    return mesh.shape["segment"] == 2 and mesh.shape["dp"] % 4 == 0
+
+
 def solution(mesh):
     placed = (
         P("dp", None),
@@ -230,5 +658,5 @@
         P("segment", "dp", None),
     )
     return jax.shard_map(
-        body, mesh=mesh, in_specs=placed, out_specs=P("segment", "dp", None), check_vma=False
-    )
+        fused_body if fits(mesh) else body, mesh=mesh, in_specs=placed, out_specs=P("segment", "dp", None), check_vma=False
+    )

time: 444 us -> 106 us (0.24)
  waiting for transfers between devices: 117 us -> 0 us
  starting transfers between devices: 110 us -> 0 us
  Pallas kernels: 0 us -> 97.2 us
  blocking collectives: 90.2 us -> 0 us
  matrix products: 43.1 us -> 0 us
  local copies, waits for them, and re-layouts: 31.9 us -> 2.99 us
  other arithmetic: 32.7 us -> 5.11 us
  between operations: 13.5 us -> 0.03 us
    ppermute x18 -> x0, starting transfers between devices: 110 us -> none  [passed_along(): return lax.ppermute(shard, axis, pairs)]
    pallas_call x0 -> x1, Pallas kernels: none -> 97.2 us  [fused_body(): pl.pallas_call(functools.partial(step_kernel, shape), out_shape=jax.Shape...]
    all_gather x2 -> x0, blocking collectives: 90.2 us -> none  [the longest x1 47.4 us: body(): lax.all_gather(w_in, 'dp', axis=1, tiled=True)]
    unnamed x2 -> x0, waiting for transfers between devices: 83 us -> none
    dot_general x34 -> x0, matrix products: 43.1 us -> none  [the longest x8 19.2 us: block_forward(): jnp.dot(activation, second, preferred_element_type=jnp.float32)]
    ppermute x18 -> x0, waiting for transfers between devices: 34.4 us -> none  [passed_along(): return lax.ppermute(shard, axis, pairs)]
    dynamic_update_slice x16 -> x0, other arithmetic: 21.7 us -> none  [put_slot(): return lax.dynamic_update_index_in_dim(buffer, value, slot_index, 0)]
    broadcast_in_dim x67 -> x2, local copies, waits for them, and re-layouts: 11.2 us -> 1.29 us  [the longest x1 1.28 us: fused_body(): reward_dir[None]]
  transfers between devices with their start and end apart: 19 -> 0, of which waited for: 19 -> 0; matrix products, arithmetic and copies ran while one was open for 0% -> 0% of each run, Pallas kernels for 0% -> 0%
where the time goes in v1:
time: 106 us; the launch traced here: 105 us
  Pallas kernels  97.2 us (92%)
  other arithmetic  5.11 us (5%)
  local copies, waits for them, and re-layouts  2.99 us (3%)
    pallas_call x1, Pallas kernels, fused_body(): pl.pallas_call(functools.partial(step_kernel, shape), out_shape=jax.Shape...  97.2 us

profile of v1, /device:TPU:0, one launch (start us, length us, event | category | flops | bytes accessed | tf_op | source)
XLA Modules:
  0.0 105.3 jit_solution(602845386046855333)
XLA Ops:
  0.0 0.1 pad.7.clone
  0.1 0.8 divide_bitcast_fusion
  0.9 0.1 subtract_bitcast_fusion
  0.9 0.6 pad_maximum_fusion.2.coef_ref
  1.5 1.3 %broadcast_in_dim.12.reward_ref = f32[1,640]{1,0:T(1,128)} reshape(f32[640]{0:T(1024)} %param.11) | data formatting | bytes 5120 | tf_op jit(solution)/shard_map/broadcast_in_dim | solution.py:641
  2.8 0.1 multiply_sine_fusion
  3.0 0.7 pad_maximum_fusion.1.embed_ref
  3.6 1.4 %maximum_maximum_fusion.param_ref = f32[8,640]{1,0:T(8,128)} fusion(f32[1,640]{1,0:T(1,128)} %param.13, f32[1,640]{1,0:T(1,128)} %param.12, f32[8]{0:T(128)S(1)} %pad.7.clone), kind=kLoop, calls=%fused_computation.1 | loop fusion | flops 10240 | bytes 25632 | tf_op jit(solution)/shard_map/concatenate | solution.py:600
  5.0 1.5 %pad_maximum_fusion.shard_ref = bf16[2,40,640]{2,1,0:T(8,128)(2,1)} fusion(bf16[1,40,640]{2,1,0:T(8,128)(2,1)} %param.15, bf16[1,40,640]{2,1,0:T(8,128)(2,1)} %param.14), kind=kLoop, calls=%fused_computation | loop fusion | flops 51200 | bytes 204800 | tf_op jit(solution)/shard_map/concatenate | solution.py:599
  6.5 97.2 %shard_map.82 = f32[40,1280]{1,0:T(8,128)} custom-call(bf16[2,40,640]{2,1,0:T(8,128)(2,1)} %pad_maximum_fusion.shard_ref, f32[8,640]{1,0:T(8,128)} %maximum_maximum_fusion.param_ref, bf16[1024,640]{1,0:T(8,128)(2,1)} %latent_ref.1, bf16[1024,640]{1,0:T(8,128)(2,1)} %noise_ref.1, f32[4,640]{1,0:T(4,128)} %pad_maximum_fusion.1.embed_ref, ...), custom_call_target="tpu_custom_call" | custom-call | tf_op jit(solution)/shard_map/pallas_call | solution.py:608
  103.7 1.6 %copy.10 = f32[1,40,1280]{2,1,0:T(8,128)} copy(f32[1,40,1280]{2,1,0:T(8,128)} %bitcast.7) | data formatting | bytes 409600
  (2 shorter events, 0.0 us)

commit v2 on v1

--- a/solution.py
+++ b/solution.py
@@ -229,10 +229,21 @@
     return jnp.concatenate([high, middle, low], axis=0).astype(jnp.bfloat16)
 
 
+class Pair:
+    def __init__(self, copies):
+        self.copies = copies
+
+    def wait_recv(self):
+        for copy in self.copies:
+            copy.wait_recv()
+
+
 def step_kernel(
     shape,
-    shard_ref,
-    param_ref,
+    win_ref,
+    wout_ref,
+    gain_ref,
+    time_ref,
     latent_ref,
     noise_ref,
     embed_ref,
@@ -243,6 +254,7 @@
     pbuf,
     weights,
     states,
+    noises,
     normed,
     slopes,
     acts,
@@ -296,6 +308,23 @@
         pending.append(copy)
         return copy
 
+    base = pl.multiple_of(core * (images * rows), images * rows)
+    locals_ = [
+        pltpu.make_async_copy(source, target, local_sem.at[k])
+        for k, (source, target) in enumerate(
+            (
+                (win_ref.at[0], wbuf.at[core, col, z, 0]),
+                (wout_ref.at[0], wbuf.at[core, col, z, 1]),
+                (gain_ref, pbuf.at[core, 0]),
+                (time_ref, pbuf.at[core, 1]),
+                (latent_ref.at[pl.ds(base, images * rows)], states.at[0]),
+                (noise_ref.at[pl.ds(base, images * rows)], noises),
+            )
+        )
+    ]
+    for copy in locals_:
+        copy.start()
+
     barrier = pltpu.get_barrier_semaphore()
     friends = [x_dev, y_dev, partner] + z_dev[1:]
     for device in friends:
@@ -304,19 +333,21 @@
         )
     pl.semaphore_wait(barrier, len(friends))
 
-    own = pltpu.make_async_copy(shard_ref, wbuf.at[core, col, z], local_sem.at[0])
-    own.start()
-    own_param = pltpu.make_async_copy(param_ref, pbuf.at[core], local_sem.at[1])
-    own_param.start()
-
-    to_z = [None] + [
-        remote(shard_ref, wbuf.at[core, col, z], z_dev[dz]) for dz in range(1, depth)
-    ]
-    to_x = [remote(shard_ref, wbuf.at[core, col, z], x_dev)]
-    to_y = [remote(shard_ref, wbuf.at[core, col, z], y_dev)]
+    def own_shard(device):
+        return Pair(
+            [
+                remote(source.at[0], wbuf.at[core, col, z, kind], device)
+                for kind, source in enumerate((win_ref, wout_ref))
+            ]
+        )
+
+    to_z = [None] + [own_shard(z_dev[dz]) for dz in range(1, depth)]
+    to_x = [own_shard(x_dev)]
+    to_y = [own_shard(y_dev)]
     to_core = [
-        remote(shard_ref, wbuf.at[core, col, z], partner),
-        remote(param_ref, pbuf.at[core], partner),
+        own_shard(partner),
+        remote(gain_ref, pbuf.at[core, 0], partner),
+        remote(time_ref, pbuf.at[core, 1], partner),
     ]
     ch = lax.broadcasted_iota(jnp.int32, gather_mat.shape, 0)
     gr = lax.broadcasted_iota(jnp.int32, gather_mat.shape, 1) * (channels // GROUPS)
@@ -350,8 +381,8 @@
         second[2 * dz + 1].wait_recv()
         piece = wbuf.at[core, qd, z_from[dz]]
         to_core.append(remote(piece, piece, partner))
-    own.wait()
-    own_param.wait()
+    for copy in locals_:
+        copy.wait()
     for copy in to_core:
         copy.wait_recv()
 
@@ -405,21 +436,10 @@
         return (block - means[stage, pl.ds(i, 1), :]) * scales[stage, pl.ds(i, 1), :]
 
     joint = 2 if images % 2 == 0 else 1
-    base = core * (images * rows)
-
-    def load_body(i, carry):
-        where = pl.ds(pl.multiple_of(i * rows, rows), rows)
-        states[0, where, :] = latent_ref[
-            pl.ds(pl.multiple_of(base + i * rows, rows), rows), :
-        ]
-        return carry
-
-    lax.fori_loop(0, images, load_body, 0)
-
     for section in range(2):
         statistics(section)
-        gain_row = pbuf[section, 0:1, :]
-        time_row = pbuf[section, 1:2, :]
+        gain_row = pbuf[section, 0]
+        time_row = pbuf[section, 1]
 
         def forward_body(g, carry):
             for j in range(joint):
@@ -457,12 +477,10 @@
         where = pl.ds(pl.multiple_of(i * rows, rows), rows)
         pred = unit(2, i)
         current = states[0, where, :].astype(jnp.float32)
-        fresh = noise_ref[pl.ds(pl.multiple_of(base + i * rows, rows), rows), :].astype(
-            jnp.float32
-        )
+        fresh = noises[where, :].astype(jnp.float32)
         keep, pull, stir = coef_ref[0, i], coef_ref[1, i], coef_ref[2, i]
         squashed = jnp.tanh(keep * current + pull * pred + stir * fresh)
-        grad = (1.0 - squashed * squashed) * (reward_ref[...] * (pull * loss_scale))
+        grad = (1.0 - squashed * squashed) * (reward_ref[...][None] * (pull * loss_scale))
         spread[where, :] = grad
         sums[pl.ds(i, 1), :] = jnp.sum(grad, axis=0, keepdims=True)
         sums[pl.ds(images + i, 1), :] = jnp.sum(grad * pred, axis=0, keepdims=True)
@@ -491,7 +509,7 @@
     pull_back(2, None)
 
     for section in (1, 0):
-        gain_row = pbuf[section, 0:1, :]
+        gain_row = pbuf[section, 0]
 
         def backward_body(g, carry):
             span = pl.ds(pl.multiple_of(g * joint * rows, rows), joint * rows)
@@ -523,57 +541,66 @@
                     owner * shard : (owner + 1) * shard
                 ]
 
-    def add(kind, q, values_ref):
-        def body(k, carry):
-            grads[core, kind, q, k] = grads[core, kind, q, k] + values_ref[k]
-            return carry
-
-        lax.fori_loop(0, depth, body, 0)
-
     order = ((qd, qd), (qx, qy), (qy, qx), (col, col))
-    swaps = {}
-    for step in range(4):
-        for kind in range(2):
-            q = order[step][kind]
-            swaps[step, kind] = remote(
-                grads.at[other, kind, q], inbox0.at[kind, q], partner
-            )
-    first = {}
-    final = {}
-    cross = ((x_dev, qx, qy), (y_dev, qy, qx))
-    for step in range(2):
-        for kind in range(2):
-            q = order[step][kind]
-            swaps[step, kind].wait_recv()
-            add(kind, q, inbox0.at[kind, q])
-            first[step, kind] = remote(
-                grads.at[core, kind, q], inbox1.at[kind, step], cross[kind][0]
-            )
-    for kind in range(2):
-        q = order[2][kind]
-        swaps[2, kind].wait_recv()
-        add(kind, q, inbox0.at[kind, q])
-        first[0, kind].wait_recv()
-        add(kind, q, inbox1.at[kind, 0])
-        final[kind] = remote(grads.at[core, kind, q], inbox2.at[kind], cross[1 - kind][0])
-    last = {}
-    for kind in range(2):
-        swaps[3, kind].wait_recv()
-        add(kind, col, inbox0.at[kind, col])
-        first[1, kind].wait_recv()
-        add(kind, col, inbox1.at[kind, 1])
-        final[kind].wait_recv()
-        add(kind, col, inbox2.at[kind])
-        for dz in range(1, depth):
-            last[kind, dz] = remote(
-                grads.at[core, kind, col, z_at[dz]], inbox3.at[kind, dz], z_dev[dz]
-            )
-    for kind in range(2):
-        total = grads[core, kind, col, z]
-        for dz in range(1, depth):
-            last[kind, dz].wait_recv()
+    cross = (x_dev, y_dev)
+    chunks = [dz for dz in range(depth - 1, 0, -1)] + [0]
+    kinds = range(2)
+    swaps, first, final, last = {}, {}, {}, {}
+
+    def mine(kind, q, dz):
+        return grads.at[core, kind, q, z_at[dz]]
+
+    def add(target, source):
+        target[...] = target[...] + source[...]
+
+    for dz in chunks:
+        for step in range(4):
+            for kind in kinds:
+                q = order[step][kind]
+                swaps[dz, step, kind] = remote(
+                    grads.at[other, kind, q, z_at[dz]], inbox0.at[kind, q, z_at[dz]], partner
+                )
+
+    def summed(dz, step, kind):
+        q = order[step][kind]
+        swaps[dz, step, kind].wait_recv()
+        add(mine(kind, q, dz), inbox0.at[kind, q, z_at[dz]])
+        return mine(kind, q, dz)
+
+    def stage_one(dz):
+        for step in range(2):
+            for kind in kinds:
+                first[dz, step, kind] = remote(
+                    summed(dz, step, kind), inbox1.at[kind, step, z_at[dz]], cross[kind]
+                )
+
+    def stage_two(dz):
+        for kind in kinds:
+            total = summed(dz, 2, kind)
+            first[dz, 0, kind].wait_recv()
+            add(total, inbox1.at[kind, 0, z_at[dz]])
+            final[dz, kind] = remote(total, inbox2.at[kind, z_at[dz]], cross[1 - kind])
+
+    def stage_three(dz):
+        for kind in kinds:
+            total = summed(dz, 3, kind)
+            first[dz, 1, kind].wait_recv()
+            add(total, inbox1.at[kind, 1, z_at[dz]])
+            final[dz, kind].wait_recv()
+            add(total, inbox2.at[kind, z_at[dz]])
+            if dz > 0:
+                last[dz, kind] = remote(total, inbox3.at[kind, dz], z_dev[dz])
+
+    for turn in range(depth + 2):
+        for lag, stage in ((0, stage_one), (1, stage_two), (2, stage_three)):
+            if 0 <= turn - lag < depth:
+                stage(chunks[turn - lag])
+    for kind in kinds:
+        total = mine(kind, col, 0)[...]
+        for dz in chunks[:-1]:
+            last[dz, kind].wait_recv()
             total = total + inbox3[kind, dz]
-        out_ref[:, kind * channels : (kind + 1) * channels] = total
+        out_ref[0, :, kind * channels : (kind + 1) * channels] = total
     for copy in pending:
         copy.wait_send()
 
@@ -596,25 +623,24 @@
     coefs = jnp.stack(
         [coef_p / coef_a, coef_q - coef_p * coef_b / coef_a, 0.5 * jnp.sqrt(1.0 - ab_prev)]
     )
-    shards = jnp.concatenate([w_in, w_out], axis=0)
-    params = jnp.concatenate([gain, time_scale, jnp.zeros((6, channels), jnp.float32)], axis=0)
     shape = (dp, depth, shard, channels, images, rows, loss_scale)
     total_rows = images * rows
     bf16, f32 = jnp.bfloat16, jnp.float32
     lines = -(-2 * images // 8) * 8
     square = (shard, channels)
-    copies = 96 * depth
+    copies = 64 * depth
     vmem = pl.BlockSpec(memory_space=pltpu.VMEM)
     grad_rows = pl.pallas_call(
         functools.partial(step_kernel, shape),
-        out_shape=jax.ShapeDtypeStruct((shard, 2 * channels), f32),
-        in_specs=[vmem] * 6 + [pl.BlockSpec(memory_space=pltpu.SMEM)],
+        out_shape=jax.ShapeDtypeStruct((1, shard, 2 * channels), f32),
+        in_specs=[vmem] * 4 + [pl.BlockSpec(memory_space=pl.ANY)] * 2 + [vmem] * 2 + [pl.BlockSpec(memory_space=pltpu.SMEM)],
         out_specs=vmem,
         scratch_shapes=[
             pltpu.VMEM((2, 4, depth, 2) + square, bf16),
-            pltpu.VMEM((2, 8, channels), f32),
+            pltpu.VMEM((2, 2, 1, channels), f32),
             pltpu.VMEM((2, 2, channels, channels), bf16),
             pltpu.VMEM((3, total_rows, channels), bf16),
+            pltpu.VMEM((total_rows, channels), bf16),
             pltpu.VMEM((2, total_rows, channels), bf16),
             pltpu.VMEM((2, total_rows, channels), f32),
             pltpu.VMEM((2, total_rows, channels), bf16),
@@ -633,13 +659,13 @@
             pltpu.VMEM((2, depth) + square, f32),
             pltpu.SemaphoreType.DMA((copies,)),
             pltpu.SemaphoreType.DMA((copies,)),
-            pltpu.SemaphoreType.DMA((2,)),
+            pltpu.SemaphoreType.DMA((6,)),
         ],
         compiler_params=pltpu.CompilerParams(
             collective_id=0, has_side_effects=True, vmem_limit_bytes=60 * 1024 * 1024
         ),
-    )(shards, params, latents, noise, embeds, reward_dir[None], coefs)
-    return grad_rows[None]
+    )(w_in, w_out, gain, time_scale, latents, noise, embeds, reward_dir, coefs)
+    return grad_rows
 
 
 def fits(mesh):

time: 106 us -> 86.1 us (0.81)
  Pallas kernels: 97.2 us -> 82 us
  other arithmetic: 5.11 us -> 2.24 us
  local copies, waits for them, and re-layouts: 2.99 us -> 1.62 us
    pallas_call x1, Pallas kernels: 97.2 us -> 82 us  [fused_body(): pl.pallas_call(functools.partial(step_kernel, shape), out_shape=jax.Shape...]
    concatenate x2 -> x0, other arithmetic: 2.85 us -> none  [the longest x1 1.48 us: fused_body(): shards = jnp.concatenate([w_in, w_out], axis=0)]
    broadcast_in_dim x2 -> x0, local copies, waits for them, and re-layouts: 1.29 us -> none  [the longest x1 1.28 us: fused_body(): reward_dir[None]]
where the time goes in v2:
time: 86.1 us; the launch traced here: 85.9 us
  Pallas kernels  82 us (95%)
  other arithmetic  2.24 us (3%)
  local copies, waits for them, and re-layouts  1.62 us (2%)
    pallas_call x1, Pallas kernels, fused_body(): pl.pallas_call(functools.partial(step_kernel, shape), out_shape=jax.Shape...  82 us

profile of v2, /device:TPU:0, one launch (start us, length us, event | category | flops | bytes accessed | tf_op | source)
XLA Modules:
  0.0 85.9 jit_solution(4442310223938943870)
XLA Ops:
  0.0 0.8 divide_bitcast_fusion
  0.8 0.1 subtract_bitcast_fusion
  0.9 0.6 pad_maximum_fusion.1.coef_ref
  1.5 0.1 multiply_sine_fusion
  1.6 0.7 pad_maximum_fusion.embed_ref
  2.3 82.0 %shard_map.82 = f32[1,40,1280]{2,1,0:T(8,128)} custom-call(bf16[1,40,640]{2,1,0:T(8,128)(2,1)} %win_ref.1, bf16[1,40,640]{2,1,0:T(8,128)(2,1)} %wout_ref.1, f32[1,640]{1,0:T(1,128)} %gain_ref.1, f32[1,640]{1,0:T(1,128)} %time_ref.1, bf16[1024,640]{1,0:T(8,128)(2,1)} %latent_ref.1, bf16[1024,640]{1,0:T(8,128)(2,1)} %noise_ref.1, ...), custom_call_target="tpu_custom_call" | custom-call | tf_op jit(solution)/shard_map/pallas_call | solution.py:633
  84.3 1.6 %copy.10 = f32[1,40,1280]{2,1,0:T(8,128)} copy(f32[1,40,1280]{2,1,0:T(8,128)} %shard_map.82) | data formatting | bytes 409600
  (1 shorter events, 0.0 us)

commit v3 on v2

--- a/solution.py
+++ b/solution.py
@@ -11,6 +11,7 @@
 GROUPS = 32
 NSTEPS = 1000
 STRIDE = 20
+LEAD = 2
 
 
 EPS = 1e-05
@@ -246,10 +247,11 @@
     time_ref,
     latent_ref,
     noise_ref,
+    times_ref,
+    reward_ref,
+    out_ref,
     embed_ref,
-    reward_ref,
     coef_ref,
-    out_ref,
     wbuf,
     pbuf,
     weights,
@@ -271,6 +273,8 @@
     inbox1,
     inbox2,
     inbox3,
+    result,
+    closed,
     send_sem,
     recv_sem,
     local_sem,
@@ -290,6 +294,7 @@
     z_at = [lax.rem(z + dz, depth) for dz in range(depth)]
     z_from = [lax.rem(z + depth - dz, depth) for dz in range(depth)]
     z_dev = [(z_at[dz] * 4 + col, core) for dz in range(depth)]
+    near = sorted(range(1, depth), key=lambda dz: (min(dz, depth - dz), dz))
     count = [0]
     pending = []
 
@@ -341,9 +346,9 @@
             ]
         )
 
-    to_z = [None] + [own_shard(z_dev[dz]) for dz in range(1, depth)]
     to_x = [own_shard(x_dev)]
     to_y = [own_shard(y_dev)]
+    to_z = {dz: own_shard(z_dev[dz]) for dz in near}
     to_core = [
         own_shard(partner),
         remote(gain_ref, pbuf.at[core, 0], partner),
@@ -359,16 +364,38 @@
     scatter_mat[...] = jnp.where(inside, 1.0, 0.0).astype(jnp.bfloat16)
     sums[...] = jnp.zeros_like(sums)
 
-    for dz in range(1, depth):
+    def column(stacked):
+        line = lax.broadcasted_iota(jnp.int32, stacked.shape, 0)
+        values = jnp.zeros(stacked.shape, jnp.float32)
+        for i in range(images):
+            values = jnp.where(
+                line == i, times_ref[core * images + i].astype(jnp.float32), values
+            )
+        return values
+
+    half_width = channels // 2
+    lane = lax.broadcasted_iota(jnp.int32, embed_ref.shape, 1)
+    k_index = jnp.where(lane < half_width, lane, lane - half_width).astype(jnp.float32)
+    phases = column(embed_ref) * jnp.exp(-math.log(10000.0) * k_index / half_width)
+    embed_ref[...] = jnp.where(lane < half_width, jnp.sin(phases), jnp.cos(phases))
+    now = column(coef_ref.at[0])
+    ab_now, ab_prev = alpha_bar(now), alpha_bar(now - STRIDE)
+    coef_a, coef_b = jnp.sqrt(ab_now), jnp.sqrt(1.0 - ab_now)
+    coef_p, coef_q = jnp.sqrt(ab_prev), jnp.sqrt(0.75 * (1.0 - ab_prev))
+    coef_ref[0] = coef_p / coef_a
+    coef_ref[1] = coef_q - coef_p * coef_b / coef_a
+    coef_ref[2] = 0.5 * jnp.sqrt(1.0 - ab_prev)
+
+    for dz in near:
         to_z[dz].wait_recv()
         piece = wbuf.at[core, col, z_from[dz]]
         to_x.append(remote(piece, piece, x_dev))
         to_y.append(remote(piece, piece, y_dev))
         to_core.append(remote(piece, piece, partner))
     second = []
-    for dz in range(depth):
-        to_x[dz].wait_recv()
-        to_y[dz].wait_recv()
+    for turn, dz in enumerate([0] + near):
+        to_x[turn].wait_recv()
+        to_y[turn].wait_recv()
         from_x = wbuf.at[core, qx, z_from[dz]]
         from_y = wbuf.at[core, qy, z_from[dz]]
         half_in, half_out = from_x.at[0], from_y.at[1]
@@ -376,9 +403,9 @@
         second.append(remote(half_out, half_out, x_dev))
         to_core.append(remote(from_x, from_x, partner))
         to_core.append(remote(from_y, from_y, partner))
-    for dz in range(depth):
-        second[2 * dz].wait_recv()
-        second[2 * dz + 1].wait_recv()
+    for turn, dz in enumerate([0] + near):
+        second[2 * turn].wait_recv()
+        second[2 * turn + 1].wait_recv()
         piece = wbuf.at[core, qd, z_from[dz]]
         to_core.append(remote(piece, piece, partner))
     for copy in locals_:
@@ -478,7 +505,7 @@
         pred = unit(2, i)
         current = states[0, where, :].astype(jnp.float32)
         fresh = noises[where, :].astype(jnp.float32)
-        keep, pull, stir = coef_ref[0, i], coef_ref[1, i], coef_ref[2, i]
+        keep, pull, stir = (coef_ref[j, pl.ds(i, 1), 0:1] for j in range(3))
         squashed = jnp.tanh(keep * current + pull * pred + stir * fresh)
         grad = (1.0 - squashed * squashed) * (reward_ref[...][None] * (pull * loss_scale))
         spread[where, :] = grad
@@ -508,99 +535,128 @@
 
     pull_back(2, None)
 
-    for section in (1, 0):
-        gain_row = pbuf[section, 0]
-
-        def backward_body(g, carry):
+    qa = qx + core * (qy - qx)
+    qb = qy + core * (qx - qy)
+    a_dev, b_dev = (z * 4 + qa, core), (z * 4 + qb, core)
+    own_order, their_order = (qd, qa, qb, col), (qd, qb, qa, col)
+    chunks = list(range(depth - 1, 0, -1)) + [0]
+    pieces = [(section, dz) for section in (1, 0) for dz in chunks]
+    swaps, first, final, last = {}, {}, {}, {}
+
+    def mine(section, q, dz):
+        return grads.at[section, core, q, z_at[dz]]
+
+    def add(target, source):
+        target[...] = target[...] + source[...]
+
+    def swap(section):
+        for dz in chunks:
+            for step in range(4):
+                q = their_order[step]
+                swaps[section, dz, step] = remote(
+                    grads.at[section, other, q, z_at[dz]],
+                    inbox0.at[section, q, z_at[dz]],
+                    partner,
+                )
+
+    def summed(section, dz, step):
+        q = own_order[step]
+        swaps[section, dz, step].wait_recv()
+        target = mine(section, q, dz)
+        add(target, inbox0.at[section, q, z_at[dz]])
+        return target
+
+    def stage_one(section, dz):
+        for step in range(2):
+            first[section, dz, step] = remote(
+                summed(section, dz, step), inbox1.at[section, step, z_at[dz]], a_dev
+            )
+
+    def stage_two(section, dz):
+        total = summed(section, dz, 2)
+        first[section, dz, 0].wait_recv()
+        add(total, inbox1.at[section, 0, z_at[dz]])
+        final[section, dz] = remote(total, inbox2.at[section, z_at[dz]], b_dev)
+
+    def stage_three(section, dz):
+        total = summed(section, dz, 3)
+        first[section, dz, 1].wait_recv()
+        add(total, inbox1.at[section, 1, z_at[dz]])
+        final[section, dz].wait_recv()
+        add(total, inbox2.at[section, z_at[dz]])
+        if dz > 0:
+            last[section, dz] = remote(total, inbox3.at[section, dz], z_dev[dz])
+
+    def turn_of(turn):
+        for lag, stage in ((0, stage_one), (LEAD, stage_two), (LEAD + 1, stage_three)):
+            if 0 <= turn - lag < len(pieces):
+                stage(*pieces[turn - lag])
+
+    def weight_grad(section, kind):
+        if kind == 0:
+            term = contract_rows(normed[section], gradpre[section])
+        else:
+            term = contract_rows(acts[section], cots[section])
+        for owner in range(dp):
+            grads[section, kind, owner % 4, owner // 4] = term[
+                owner * shard : (owner + 1) * shard
+            ]
+
+    def grad_preact(section):
+        def body(g, carry):
             span = pl.ds(pl.multiple_of(g * joint * rows, rows), joint * rows)
             product = contract_cols(cots[section, span, :], weights[section, 1])
             gradpre[section, span, :] = (product * slopes[section, span, :]).astype(jnp.bfloat16)
-            if section > 0:
-                product = contract_cols(gradpre[section, span, :], weights[section, 0])
-                for j in range(joint):
-                    i = g * joint + j
-                    where = pl.ds(pl.multiple_of(i * rows, rows), rows)
-                    grad = product[j * rows : (j + 1) * rows] * gain_row
-                    spread[where, :] = grad
-                    sums[pl.ds(i, 1), :] = jnp.sum(grad, axis=0, keepdims=True)
-                    sums[pl.ds(images + i, 1), :] = jnp.sum(
-                        grad * unit(section, i), axis=0, keepdims=True
-                    )
             return carry
 
-        lax.fori_loop(0, images // joint, backward_body, 0)
-        if section > 0:
-            pull_back(section, section)
-        for kind in range(2):
-            if kind == 0:
-                term = contract_rows(normed[section], gradpre[section])
-            else:
-                term = contract_rows(acts[section], cots[section])
-            for owner in range(dp):
-                grads[section, kind, owner % 4, owner // 4] = term[
-                    owner * shard : (owner + 1) * shard
-                ]
-
-    order = ((qd, qd), (qx, qy), (qy, qx), (col, col))
-    cross = (x_dev, y_dev)
-    chunks = [dz for dz in range(depth - 1, 0, -1)] + [0]
-    kinds = range(2)
-    swaps, first, final, last = {}, {}, {}, {}
-
-    def mine(kind, q, dz):
-        return grads.at[core, kind, q, z_at[dz]]
-
-    def add(target, source):
-        target[...] = target[...] + source[...]
-
-    for dz in chunks:
-        for step in range(4):
-            for kind in kinds:
-                q = order[step][kind]
-                swaps[dz, step, kind] = remote(
-                    grads.at[other, kind, q, z_at[dz]], inbox0.at[kind, q, z_at[dz]], partner
+        lax.fori_loop(0, images // joint, body, 0)
+
+    def grad_normed(section):
+        gain_row = pbuf[section, 0]
+
+        def body(g, carry):
+            span = pl.ds(pl.multiple_of(g * joint * rows, rows), joint * rows)
+            product = contract_cols(gradpre[section, span, :], weights[section, 0])
+            for j in range(joint):
+                i = g * joint + j
+                where = pl.ds(pl.multiple_of(i * rows, rows), rows)
+                grad = product[j * rows : (j + 1) * rows] * gain_row
+                spread[where, :] = grad
+                sums[pl.ds(i, 1), :] = jnp.sum(grad, axis=0, keepdims=True)
+                sums[pl.ds(images + i, 1), :] = jnp.sum(
+                    grad * unit(section, i), axis=0, keepdims=True
                 )
-
-    def summed(dz, step, kind):
-        q = order[step][kind]
-        swaps[dz, step, kind].wait_recv()
-        add(mine(kind, q, dz), inbox0.at[kind, q, z_at[dz]])
-        return mine(kind, q, dz)
-
-    def stage_one(dz):
-        for step in range(2):
-            for kind in kinds:
-                first[dz, step, kind] = remote(
-                    summed(dz, step, kind), inbox1.at[kind, step, z_at[dz]], cross[kind]
-                )
-
-    def stage_two(dz):
-        for kind in kinds:
-            total = summed(dz, 2, kind)
-            first[dz, 0, kind].wait_recv()
-            add(total, inbox1.at[kind, 0, z_at[dz]])
-            final[dz, kind] = remote(total, inbox2.at[kind, z_at[dz]], cross[1 - kind])
-
-    def stage_three(dz):
-        for kind in kinds:
-            total = summed(dz, 3, kind)
-            first[dz, 1, kind].wait_recv()
-            add(total, inbox1.at[kind, 1, z_at[dz]])
-            final[dz, kind].wait_recv()
-            add(total, inbox2.at[kind, z_at[dz]])
-            if dz > 0:
-                last[dz, kind] = remote(total, inbox3.at[kind, dz], z_dev[dz])
-
-    for turn in range(depth + 2):
-        for lag, stage in ((0, stage_one), (1, stage_two), (2, stage_three)):
-            if 0 <= turn - lag < depth:
-                stage(chunks[turn - lag])
-    for kind in kinds:
-        total = mine(kind, col, 0)[...]
+            return carry
+
+        lax.fori_loop(0, images // joint, body, 0)
+
+    grad_preact(1)
+    weight_grad(1, 1)
+    weight_grad(1, 0)
+    swap(1)
+    grad_normed(1)
+    turn_of(0)
+    pull_back(1, 1)
+    turn_of(1)
+    grad_preact(0)
+    turn_of(2)
+    weight_grad(0, 1)
+    turn_of(3)
+    weight_grad(0, 0)
+    swap(0)
+    for turn in range(4, len(pieces) + LEAD + 1):
+        turn_of(turn)
+    for section in (1, 0):
+        total = mine(section, col, 0)[...]
         for dz in chunks[:-1]:
-            last[dz, kind].wait_recv()
-            total = total + inbox3[kind, dz]
-        out_ref[0, :, kind * channels : (kind + 1) * channels] = total
+            last[section, dz].wait_recv()
+            total = total + inbox3[section, dz]
+        result[section] = total
+    closing = remote(result.at[other], closed, partner)
+    closing.wait_recv()
+    ours, theirs = result[core], closed[...]
+    out_ref[0, :, :channels] = jnp.where(core == 0, ours, theirs)
+    out_ref[0, :, channels:] = jnp.where(core == 0, theirs, ours)
     for copy in pending:
         copy.wait_send()
 
@@ -608,21 +664,12 @@
 def fused_body(latents, noise, timesteps, reward_dir, gain, time_scale, w_in, w_out):
     dp = lax.axis_size("dp")
     depth = dp // 4
-    core = lax.axis_index("segment")
     micro_count = timesteps.shape[0]
     images = micro_count // 2
     rows = latents.shape[0] // micro_count
     channels = latents.shape[1]
     shard = w_in.shape[1]
     loss_scale = 1.0 / math.sqrt(dp * latents.shape[0])
-    times = lax.dynamic_slice_in_dim(timesteps, core * images, images)
-    embeds = jax.vmap(lambda values: time_embed(values, channels))(times)
-    ab_now, ab_prev = alpha_bar(times), alpha_bar(times - STRIDE)
-    coef_a, coef_b = jnp.sqrt(ab_now), jnp.sqrt(1.0 - ab_now)
-    coef_p, coef_q = jnp.sqrt(ab_prev), jnp.sqrt(0.75 * (1.0 - ab_prev))
-    coefs = jnp.stack(
-        [coef_p / coef_a, coef_q - coef_p * coef_b / coef_a, 0.5 * jnp.sqrt(1.0 - ab_prev)]
-    )
     shape = (dp, depth, shard, channels, images, rows, loss_scale)
     total_rows = images * rows
     bf16, f32 = jnp.bfloat16, jnp.float32
@@ -633,9 +680,12 @@
     grad_rows = pl.pallas_call(
         functools.partial(step_kernel, shape),
         out_shape=jax.ShapeDtypeStruct((1, shard, 2 * channels), f32),
-        in_specs=[vmem] * 4 + [pl.BlockSpec(memory_space=pl.ANY)] * 2 + [vmem] * 2 + [pl.BlockSpec(memory_space=pltpu.SMEM)],
+        in_specs=[vmem] * 4 + [pl.BlockSpec(memory_space=pl.ANY)] * 2
+        + [pl.BlockSpec(memory_space=pltpu.SMEM), vmem],
         out_specs=vmem,
         scratch_shapes=[
+            pltpu.VMEM((-(-images // 8) * 8, channels), f32),
+            pltpu.VMEM((3, -(-images // 8) * 8, 128), f32),
             pltpu.VMEM((2, 4, depth, 2) + square, bf16),
             pltpu.VMEM((2, 2, 1, channels), f32),
             pltpu.VMEM((2, 2, channels, channels), bf16),
@@ -657,6 +707,8 @@
             pltpu.VMEM((2, 2, depth) + square, f32),
             pltpu.VMEM((2, depth) + square, f32),
             pltpu.VMEM((2, depth) + square, f32),
+            pltpu.VMEM((2,) + square, f32),
+            pltpu.VMEM(square, f32),
             pltpu.SemaphoreType.DMA((copies,)),
             pltpu.SemaphoreType.DMA((copies,)),
             pltpu.SemaphoreType.DMA((6,)),
@@ -664,12 +716,12 @@
         compiler_params=pltpu.CompilerParams(
             collective_id=0, has_side_effects=True, vmem_limit_bytes=60 * 1024 * 1024
         ),
-    )(w_in, w_out, gain, time_scale, latents, noise, embeds, reward_dir, coefs)
+    )(w_in, w_out, gain, time_scale, latents, noise, timesteps, reward_dir)
     return grad_rows
 
 
 def fits(mesh):
-    return mesh.shape["segment"] == 2 and mesh.shape["dp"] % 4 == 0
+    return mesh.shape["segment"] == 2 and mesh.shape["dp"] % 4 == 0 and mesh.shape["dp"] >= 16
 
 
 def solution(mesh):

time: 86.1 us -> 79.9 us (0.928)
  Pallas kernels: 82 us -> 78 us
  other arithmetic: 2.24 us -> 0 us
    pallas_call x1, Pallas kernels: 82 us -> 78 us  [fused_body(): pl.pallas_call(functools.partial(step_kernel, shape), out_shape=jax.Shape...]
    another operation x3 -> x0, other arithmetic: 1.43 us -> none  [fused_body(): jnp.stack([coef_p / coef_a, coef_q - coef_p * coef_b / coef_a, 0.5 * jnp....]
where the time goes in v3:
time: 79.9 us; the launch traced here: 79.7 us
  Pallas kernels  78 us (98%)
  local copies, waits for them, and re-layouts  1.62 us (2%)
    pallas_call x1, Pallas kernels, fused_body(): pl.pallas_call(functools.partial(step_kernel, shape), out_shape=jax.Shape...  78 us
    unnamed x1, local copies, waits for them, and re-layouts  1.62 us

profile of v3, /device:TPU:0, one launch (start us, length us, event | category | flops | bytes accessed | tf_op | source)
XLA Modules:
  0.0 79.7 jit_solution(8275052385807028176)
XLA Ops:
  0.0 78.0 %shard_map.82 = f32[1,40,1280]{2,1,0:T(8,128)} custom-call(bf16[1,40,640]{2,1,0:T(8,128)(2,1)} %win_ref.1, bf16[1,40,640]{2,1,0:T(8,128)(2,1)} %wout_ref.1, f32[1,640]{1,0:T(1,128)} %gain_ref.1, f32[1,640]{1,0:T(1,128)} %time_ref.1, bf16[1024,640]{1,0:T(8,128)(2,1)} %latent_ref.1, bf16[1024,640]{1,0:T(8,128)(2,1)} %noise_ref.1, s32[8]{0:T(128)} %times_ref.1, ...), custom_call_target="tpu_custom_call" | custom-call | tf_op jit(solution)/shard_map/pallas_call | solution.py:680
  78.1 1.6 %copy.10 = f32[1,40,1280]{2,1,0:T(8,128)} copy(f32[1,40,1280]{2,1,0:T(8,128)} %shard_map.82) | data formatting | bytes 409600

commit v4 on v3

--- a/solution.py
+++ b/solution.py
@@ -234,9 +234,17 @@
     def __init__(self, copies):
         self.copies = copies
 
+    def start(self):
+        for copy in self.copies:
+            copy.start()
+
     def wait_recv(self):
         for copy in self.copies:
             copy.wait_recv()
+
+    def wait_send(self):
+        for copy in self.copies:
+            copy.wait_send()
 
 
 def step_kernel(
@@ -294,11 +302,10 @@
     z_at = [lax.rem(z + dz, depth) for dz in range(depth)]
     z_from = [lax.rem(z + depth - dz, depth) for dz in range(depth)]
     z_dev = [(z_at[dz] * 4 + col, core) for dz in range(depth)]
-    near = sorted(range(1, depth), key=lambda dz: (min(dz, depth - dz), dz))
     count = [0]
     pending = []
 
-    def remote(src, dst, device):
+    def reserve(src, dst, device):
         k = count[0]
         count[0] += 1
         copy = pltpu.make_async_remote_copy(
@@ -309,6 +316,10 @@
             device_id=device,
             device_id_type=pl.DeviceIdType.MESH,
         )
+        return copy
+
+    def remote(src, dst, device):
+        copy = reserve(src, dst, device)
         copy.start()
         pending.append(copy)
         return copy
@@ -346,9 +357,31 @@
             ]
         )
 
-    to_x = [own_shard(x_dev)]
-    to_y = [own_shard(y_dev)]
-    to_z = {dz: own_shard(z_dev[dz]) for dz in near}
+    slots = [(way, hop) for hop in range(depth - 1) for way in (1, -1)]
+
+    def holds(way, hop):
+        return z >= hop + 1 if way > 0 else z <= depth - 2 - hop
+
+    def goes_on(way):
+        return z <= depth - 2 if way > 0 else z >= 1
+
+    def along(way):
+        return (lax.rem(z + depth + way, depth) * 4 + col, core)
+
+    own_x, own_y = own_shard(x_dev), own_shard(y_dev)
+    line = {}
+    for way in (1, -1):
+        line[way, 0] = Pair(
+            [
+                reserve(source.at[0], wbuf.at[core, col, z, kind], along(way))
+                for kind, source in enumerate((win_ref, wout_ref))
+            ]
+        )
+
+        @pl.when(goes_on(way))
+        def _(way=way):
+            line[way, 0].start()
+
     to_core = [
         own_shard(partner),
         remote(gain_ref, pbuf.at[core, 0], partner),
@@ -386,28 +419,78 @@
     coef_ref[1] = coef_q - coef_p * coef_b / coef_a
     coef_ref[2] = 0.5 * jnp.sqrt(1.0 - ab_prev)
 
-    for dz in near:
-        to_z[dz].wait_recv()
-        piece = wbuf.at[core, col, z_from[dz]]
-        to_x.append(remote(piece, piece, x_dev))
-        to_y.append(remote(piece, piece, y_dev))
-        to_core.append(remote(piece, piece, partner))
-    second = []
-    for turn, dz in enumerate([0] + near):
-        to_x[turn].wait_recv()
-        to_y[turn].wait_recv()
-        from_x = wbuf.at[core, qx, z_from[dz]]
-        from_y = wbuf.at[core, qy, z_from[dz]]
-        half_in, half_out = from_x.at[0], from_y.at[1]
-        second.append(remote(half_in, half_in, y_dev))
-        second.append(remote(half_out, half_out, x_dev))
-        to_core.append(remote(from_x, from_x, partner))
-        to_core.append(remote(from_y, from_y, partner))
-    for turn, dz in enumerate([0] + near):
-        second[2 * turn].wait_recv()
-        second[2 * turn + 1].wait_recv()
-        piece = wbuf.at[core, qd, z_from[dz]]
-        to_core.append(remote(piece, piece, partner))
+    spread_x, spread_y, diag, core_sends = {}, {}, {}, {}
+
+    def slot_piece(way, hop, q):
+        return wbuf.at[core, q, lax.rem(z + depth - way * (hop + 1), depth)]
+
+    for way, hop in slots:
+        piece = slot_piece(way, hop, col)
+        spread_x[way, hop] = reserve(piece, piece, x_dev)
+        spread_y[way, hop] = reserve(piece, piece, y_dev)
+        more = [reserve(piece, piece, partner)]
+        if hop + 1 < depth - 1:
+            line[way, hop + 1] = reserve(piece, piece, along(way))
+        core_sends[way, hop] = more
+
+        @pl.when(holds(way, hop))
+        def _(way=way, hop=hop, more=more):
+            line[way, hop].wait_recv()
+            if hop + 1 < depth - 1:
+
+                @pl.when(goes_on(way))
+                def _():
+                    line[way, hop + 1].start()
+
+            spread_x[way, hop].start()
+            spread_y[way, hop].start()
+            more[0].start()
+
+    def forward(from_x, from_y, maker):
+        return [
+            maker(from_x.at[0], from_x.at[0], y_dev),
+            maker(from_y.at[1], from_y.at[1], x_dev),
+            maker(from_x, from_x, partner),
+            maker(from_y, from_y, partner),
+        ]
+
+    own_x.wait_recv()
+    own_y.wait_recv()
+    own_diag = forward(wbuf.at[core, qx, z], wbuf.at[core, qy, z], remote)
+    to_core += own_diag[2:]
+    for way, hop in slots:
+        batch = forward(slot_piece(way, hop, qx), slot_piece(way, hop, qy), reserve)
+        diag[way, hop] = batch[:2]
+        core_sends[way, hop] += batch[2:]
+
+        @pl.when(holds(way, hop))
+        def _(way=way, hop=hop, batch=batch):
+            spread_x[way, hop].wait_recv()
+            spread_y[way, hop].wait_recv()
+            for copy in batch:
+                copy.start()
+
+    for copy in own_diag[:2]:
+        copy.wait_recv()
+    to_core.append(remote(wbuf.at[core, qd, z], wbuf.at[core, qd, z], partner))
+    for way, hop in slots:
+        piece = slot_piece(way, hop, qd)
+        closing_copy = reserve(piece, piece, partner)
+        core_sends[way, hop].append(closing_copy)
+
+        @pl.when(holds(way, hop))
+        def _(way=way, hop=hop, closing_copy=closing_copy):
+            for copy in diag[way, hop]:
+                copy.wait_recv()
+            closing_copy.start()
+
+    for way, hop in slots:
+
+        @pl.when(holds(way, hop))
+        def _(way=way, hop=hop):
+            for copy in core_sends[way, hop]:
+                copy.wait_recv()
+
     for copy in locals_:
         copy.wait()
     for copy in to_core:
@@ -659,6 +742,24 @@
     out_ref[0, :, channels:] = jnp.where(core == 0, theirs, ours)
     for copy in pending:
         copy.wait_send()
+    for way in (1, -1):
+
+        @pl.when(goes_on(way))
+        def _(way=way):
+            line[way, 0].wait_send()
+
+    for way, hop in slots:
+
+        @pl.when(holds(way, hop))
+        def _(way=way, hop=hop):
+            sent = [spread_x[way, hop], spread_y[way, hop]] + diag[way, hop]
+            for copy in sent + core_sends[way, hop]:
+                copy.wait_send()
+            if hop + 1 < depth - 1:
+
+                @pl.when(goes_on(way))
+                def _():
+                    line[way, hop + 1].wait_send()
 
 
 def fused_body(latents, noise, timesteps, reward_dir, gain, time_scale, w_in, w_out):

time: 79.9 us -> 78.8 us (0.986)
  Pallas kernels: 78 us -> 77 us
    pallas_call x1, Pallas kernels: 78 us -> 77 us  [fused_body(): pl.pallas_call(functools.partial(step_kernel, shape), out_shape=jax.Shape...]
where the time goes in v4:
time: 78.8 us; the launch traced here: 78.6 us
  Pallas kernels  77 us (98%)
  local copies, waits for them, and re-layouts  1.62 us (2%)
    pallas_call x1, Pallas kernels, fused_body(): pl.pallas_call(functools.partial(step_kernel, shape), out_shape=jax.Shape...  77 us
    unnamed x1, local copies, waits for them, and re-layouts  1.62 us

profile of v4, /device:TPU:0, one launch (start us, length us, event | category | flops | bytes accessed | tf_op | source)
XLA Modules:
  0.0 78.6 jit_solution(3539655478938852411)
XLA Ops:
  0.0 77.0 %shard_map.82 = f32[1,40,1280]{2,1,0:T(8,128)} custom-call(bf16[1,40,640]{2,1,0:T(8,128)(2,1)} %win_ref.1, bf16[1,40,640]{2,1,0:T(8,128)(2,1)} %wout_ref.1, f32[1,640]{1,0:T(1,128)} %gain_ref.1, f32[1,640]{1,0:T(1,128)} %time_ref.1, bf16[1024,640]{1,0:T(8,128)(2,1)} %latent_ref.1, bf16[1024,640]{1,0:T(8,128)(2,1)} %noise_ref.1, s32[8]{0:T(128)} %times_ref.1, ...), custom_call_target="tpu_custom_call" | custom-call | tf_op jit(solution)/shard_map/pallas_call | solution.py:781
  77.0 1.6 %copy.10 = f32[1,40,1280]{2,1,0:T(8,128)} copy(f32[1,40,1280]{2,1,0:T(8,128)} %shard_map.82) | data formatting | bytes 409600
